TPU v7x, 32 devices: a whole 2x2x4 slice. The times are simulated.
32 devices in a mesh: groups: 2 (over y), tm: 16 (over z, x, core).
Axes of the slice: x: 2, y: 2, z: 4, core: 2. Of those that a mesh axis runs over, the one named last changes fastest.
Arguments:
- noisy: bfloat16 [256, 16, 16, 256], P(('groups', 'tm')), parts along dimension 0, may hold values from -6 to 6
- observed: float32 [256, 16, 256], P(('groups', 'tm')), parts along dimension 0, may hold values from -6 to 6
- obs_mask: int32 [256, 16, 256], P(('groups', 'tm')), parts along dimension 0, may hold values 0 or 1
- obs_channel: int32 [256, 16, 256], P(('groups', 'tm')), parts along dimension 0, may hold values from 0 to 15
- step_index: int32 [2], P('groups'), parts along dimension 0, may hold values from 0 to 63
- w_first: bfloat16 [128, 80, 3, 3], replicated, may hold values from -0.21875 to 0.21875
- b_first: float32 [128], replicated, may hold values from -3 to 3
- w_second: bfloat16 [16, 128, 3, 3], replicated, may hold values from -0.1875 to 0.1875
- b_second: float32 [16], replicated, may hold values from -3 to 3
Outputs:
- guided: float32 [256, 16, 16, 256], P(('groups', 'tm')), parts along dimension 0
There are 2 independent parts, one for each index of `groups`. A program takes and returns all parts, laid end to end along the dimension named above; an argument that names none is the same for every part. Nothing has to cross between parts.
All inputs are finite; a program needn't handle non-finite values. No bound on the sum of `obs_mask` on one device may be relied on, other than what follows from the above.
Results may differ from a plain program's by a relative error of at most 0.0015.
Values may be sent and summed in bfloat16 or wider, within the bound.
No kernel may reach another device: no remote copies, remote signals or barrier semaphores. Data moves between devices by JAX's collectives and lax.ppermute only.
A program may use at most 128 MiB of HBM per device.

v0:
```python
import jax
import jax.numpy as jnp
from jax import lax
from jax.sharding import PartitionSpec as P

STEPS = 64
ROWS = 16
COLS = 256


sigma_low = 0.1
sigma_ratio = 20.0


def with_halo(x, sides, width):
    for axis, dim in sides:
        peers, length = (lax.axis_size(axis), x.shape[dim])
        up = [(i, (i + 1) % peers) for i in range(peers - 1)]
        down = [(j, i) for i, j in up]
        last = lax.slice_in_dim(x, length - width, length, axis=dim)
        initial = lax.slice_in_dim(x, 0, width, axis=dim)
        before = lax.ppermute(last, axis, up)
        after = lax.ppermute(initial, axis, down)
        x = jnp.concatenate([before, x, after], axis=dim)
    return x


def passed_along(value, axis, steps):
    count = lax.axis_size(axis)
    initial, last = (max(0, -steps), min(count, count - steps))
    return lax.ppermute(value, axis, [(source, source + steps) for source in range(initial, last)])


def conv(value, kernel):
    return lax.conv_general_dilated(
        value,
        kernel,
        (1, 1),
        ((1, 1), (1, 1)),
        dimension_numbers=("NCHW", "OIHW", "NCHW"),
        preferred_element_type=jnp.float32,
    )


def conv_back(grad, kernel):
    flipped = jnp.transpose(kernel, (1, 0, 2, 3))[:, :, ::-1, ::-1]
    return conv(grad, flipped)


def stack_windows(source, frames, span):
    return jnp.concatenate([source[k : k + frames] for k in range(span)], axis=1)


def per_device(
    noisy, observed, obs_mask, obs_channel, step_index, w_first, b_first, w_second, b_second
):
    frames = noisy.shape[0]
    chans = noisy.shape[1]
    span = w_first.shape[1] // chans
    level = step_index[0].astype(jnp.float32) / jnp.float32(STEPS - 1)
    sigma = jnp.float32(sigma_low) * jnp.exp(jnp.log(jnp.float32(sigma_ratio)) * level)
    c_in = 1.0 / jnp.sqrt(1.0 + sigma * sigma)
    weight_obs = 1.0 / (1.0 + sigma * sigma)
    scaled = (c_in * noisy.astype(jnp.float32)).astype(jnp.bfloat16)
    extended = with_halo(scaled, (("tm", 0),), 2)
    pre = conv(stack_windows(extended, frames, span), w_first)
    pre = pre + b_first[None, :, None, None]
    hidden = jax.nn.silu(pre).astype(jnp.bfloat16)
    den = noisy.astype(jnp.float32) + conv(hidden, w_second) + b_second[None, :, None, None]
    channel_ids = jnp.arange(chans, dtype=jnp.int32)
    select = (
        (obs_channel[:, None, :, :] == channel_ids[None, :, None, None])
        & (obs_mask[:, None, :, :] == 1)
    ).astype(jnp.float32)
    misfit = select * (den - observed[:, None, :, :])
    misfit_b = misfit.astype(jnp.bfloat16)
    sig = jax.nn.sigmoid(pre)
    grad_hidden = (conv_back(misfit_b, w_second) * (sig * (1.0 + pre * (1.0 - sig)))).astype(
        jnp.bfloat16
    )
    grad_window = conv_back(grad_hidden, w_first).reshape(frames, span, chans, ROWS, COLS)
    back_pad = jnp.zeros((frames + 4, chans, ROWS, COLS), jnp.float32)
    for k in range(span):
        back_pad = back_pad.at[k : k + frames].add(grad_window[:, k])
    from_right = passed_along(back_pad[:2].astype(jnp.bfloat16), "tm", -1).astype(jnp.float32)
    from_left = passed_along(back_pad[frames + 2 :].astype(jnp.bfloat16), "tm", 1).astype(
        jnp.float32
    )
    back = back_pad[2 : frames + 2]
    back = back.at[frames - 2 :].add(from_right)
    back = back.at[:2].add(from_left)
    return den - weight_obs * (misfit + c_in * back)


def solution(mesh):
    return jax.shard_map(
        per_device,
        mesh=mesh,
        in_specs=(
            P(("groups", "tm"), None, None, None),
            P(("groups", "tm"), None, None),
            P(("groups", "tm"), None, None),
            P(("groups", "tm"), None, None),
            P("groups"),
            P(),
            P(),
            P(),
            P(),
        ),
        out_specs=P(("groups", "tm"), None, None, None),
        check_vma=False,
    )
```

profile of v0, /device:TPU:1, one launch (start us, length us, event | category | flops | bytes accessed | tf_op | source)
XLA Modules:
  0.0 169.3 jit_solution(11622179099909798081)
XLA Ops:
  0.8 1.4 fusion.1
  2.3 4.6 %collective-permute-start = (bf16[2,16,16,256]{3,2,1,0:T(8,128)(2,1)S(1)}, bf16[2,16,16,256]{3,2,1,0:T(8,128)(2,1)S(1)}, u32[]{:S(2)}, u32[]{:S(2)}) collective-permute-start(bf16[2,16,16,256]{3,2,1,0:T(8,128)(2,1)S(1)} %get-tuple-element.90), channel_id=1, source_target_pairs={{0,1},{1,2},{2,3},{3,4},{4,5},{5,6},{6,7},{7,8},{8,9},{9,10},{10,1... | collective-permute-start | bytes 786440 | tf_op jit(solution)/shard_map/ppermute | solution.py:22
  6.9 1.9 %collective-permute-start.1 = (bf16[2,16,16,256]{3,2,1,0:T(8,128)(2,1)S(1)}, bf16[2,16,16,256]{3,2,1,0:T(8,128)(2,1)S(1)}, u32[]{:S(2)}, u32[]{:S(2)}) collective-permute-start(bf16[2,16,16,256]{3,2,1,0:T(8,128)(2,1)S(1)} %get-tuple-element.89), channel_id=1, source_target_pairs={{1,0},{2,1},{3,2},{4,3},{5,4},{6,5},{7,6},{8,7},{9,8},{10,9},{11,1... | collective-permute-start | bytes 786440 | tf_op jit(solution)/shard_map/ppermute | solution.py:23
  8.9 1.3 collective-permute-done
  11.3 1.1 fusion.17
  12.4 1.2 constant_dynamic-update-slice_fusion
  16.8 9.0 %copy.51 = bf16[8,80,16,256]{1,0,3,2:T(8,128)(2,1)} copy(bf16[8,80,16,256]{3,2,1,0:T(8,128)(2,1)} %fusion.16) | data formatting | bytes 10485760 | tf_op jit(solution)/shard_map/concatenate | solution.py:51
  25.8 23.8 %fusion.22 = f32[8,128,16,256]{1,0,3,2:T(8,128)S(1)} fusion(bf16[8,80,16,256]{1,0,3,2:T(8,128)(2,1)} %copy.51, bf16[128,80,3,3]{0,1,3,2:T(8,128)(2,1)S(1)} %copy-done), kind=kOutput, calls=%fused_computation.48 | convolution fusion | flops 5773066240 | bytes 22204416 | tf_op jit(solution)/shard_map/conv_general_dilated | solution.py:35
  49.6 5.7 %copy-done.9 = f32[8,128,16,256]{1,0,3,2:T(8,128)} copy-done((f32[8,128,16,256]{1,0,3,2:T(8,128)}, f32[8,128,16,256]{1,0,3,2:T(8,128)S(1)}, u32[]{:S(2)}) %copy-start.9) | copy-done | bytes 16777240
  55.3 22.4 %fusion = f32[8,16,16,256]{1,0,3,2:T(8,128)} fusion(bf16[16,128,3,3]{1,0,3,2:T(8,128)(2,1)S(1)} %copy-done.7, f32[8,128,16,256]{1,0,3,2:T(8,128)S(1)} %fusion.22, f32[128]{0:T(128)S(1)} %copy-done.8), kind=kOutput, calls=%fused_computation.3 | convolution fusion | flops 1179779072 | bytes 18911744 | tf_op jit(solution)/shard_map/conv_general_dilated | solution.py:35
  77.7 8.2 %copy.52 = f32[8,16,16,256]{3,2,1,0:T(8,128)S(1)} copy(f32[8,16,16,256]{1,0,3,2:T(8,128)} %fusion) | data formatting | bytes 4194304 | tf_op jit(solution)/shard_map/conv_general_dilated | solution.py:35
  86.0 2.6 %fusion.10 = bf16[8,16,16,256]{3,2,1,0:T(8,128)(2,1)} fusion(f32[8,16,16,256]{3,2,1,0:T(8,128)S(1)} %copy.52, bf16[8,16,16,256]{3,2,1,0:T(8,128)(2,1)S(1)} %copy-done.2, f32[8,16,256]{2,1,0:T(8,128)S(1)} %copy-done.3, s32[8,16,256]{2,1,0:T(8,128)} %param.26, f32[16]{0:T(128)S(1)} %copy-done.6, pred[8,16,256]{2,1,0:T(8,128)(4,1)S(1)} %broadcast_compare_fusion), kind=kLoop, calls=%fused_computation.22 | loop fusion | flops 4194304 | bytes 4489280 | tf_op jit(solution)/shard_map/convert_element_type | solution.py:76
  88.6 7.5 %copy.53 = bf16[8,16,16,256]{1,0,3,2:T(8,128)(2,1)} copy(bf16[8,16,16,256]{3,2,1,0:T(8,128)(2,1)} %fusion.10) | data formatting | bytes 2097152 | tf_op jit(solution)/shard_map/convert_element_type | solution.py:76
  96.1 16.5 %multiply_convert_fusion = bf16[8,128,16,256]{1,0,3,2:T(8,128)(2,1)S(1)} fusion(f32[8,128,16,256]{1,0,3,2:T(8,128)} %copy-done.9, bf16[8,16,16,256]{1,0,3,2:T(8,128)(2,1)} %copy.53, bf16[16,128,3,3]{1,0,3,2:T(8,128)(2,1)S(1)} %copy-done.7, f32[128]{0:T(128)S(1)} %copy-done.8), kind=kOutput, calls=%fused_computation | convolution fusion | flops 1196556288 | bytes 26251776 | tf_op jit(solution)/shard_map/conv_general_dilated | solution.py:35
  112.5 22.2 %fusion.23 = f32[8,80,16,256]{1,0,3,2:T(8,128)} fusion(bf16[8,128,16,256]{1,0,3,2:T(8,128)(2,1)S(1)} %multiply_convert_fusion, bf16[128,80,3,3]{0,1,3,2:T(8,128)(2,1)S(1)} %copy-done), kind=kOutput, calls=%fused_computation.49 | convolution fusion | flops 5773066240 | bytes 19058688 | tf_op jit(solution)/shard_map/conv_general_dilated | solution.py:35
  134.7 11.8 %copy.54 = f32[8,80,16,256]{3,2,1,0:T(8,128)} copy(f32[8,80,16,256]{1,0,3,2:T(8,128)} %fusion.23) | data formatting | bytes 20971520 | tf_op jit(solution)/shard_map/conv_general_dilated | solution.py:35
  146.5 1.8 %slice_bitcast_fusion.4 = f32[8,16,16,256]{3,2,1,0:T(8,128)S(1)} fusion(f32[8,5,16,16,256]{4,3,2,1,0:T(8,128)} %bitcast.44), kind=kLoop, calls=%fused_computation.19 | loop fusion | bytes 4194304 | tf_op jit(solution)/shard_map/add | solution.py:84
  148.7 2.3 %fusion.9 = f32[12,16,16,256]{3,2,1,0:T(8,128)S(1)} fusion(f32[12,16,16,256]{3,2,1,0:T(8,128)S(1)} %scatter-add.24, f32[8,5,16,16,256]{4,3,2,1,0:T(8,128)} %bitcast.45), kind=kLoop, calls=%fused_computation.18 | loop fusion | flops 524288 | bytes 6291456 | tf_op jit(solution)/shard_map/scatter-add | solution.py:84
  151.0 1.9 %copy-done.1 = f32[8,80,16,256]{3,2,1,0:T(8,128)S(1)} copy-done((f32[8,80,16,256]{3,2,1,0:T(8,128)S(1)}, f32[8,80,16,256]{3,2,1,0:T(8,128)}, u32[]{:S(2)}) %copy-start.1) | copy-done | bytes 10485784
  154.9 1.9 %collective-permute-start.2 = (bf16[2,16,16,256]{3,2,1,0:T(8,128)(2,1)S(1)}, bf16[2,16,16,256]{3,2,1,0:T(8,128)(2,1)S(1)}, u32[]{:S(2)}, u32[]{:S(2)}) collective-permute-start(bf16[2,16,16,256]{3,2,1,0:T(8,128)(2,1)S(1)} %slice.338), channel_id=1, source_target_pairs={{1,0},{2,1},{3,2},{4,3},{5,4},{6,5},{7,6},{8,7},{9,8},{10,9},{11,1... | collective-permute-start | bytes 786440 | tf_op jit(solution)/shard_map/ppermute | solution.py:31
  156.9 3.6 %collective-permute-start.3 = (bf16[2,16,16,256]{3,2,1,0:T(8,128)(2,1)S(1)}, bf16[2,16,16,256]{3,2,1,0:T(8,128)(2,1)S(1)}, u32[]{:S(2)}, u32[]{:S(2)}) collective-permute-start(bf16[2,16,16,256]{3,2,1,0:T(8,128)(2,1)S(1)} %slice.337), channel_id=1, source_target_pairs={{0,1},{1,2},{2,3},{3,4},{4,5},{5,6},{6,7},{7,8},{8,9},{9,10},{10,1... | collective-permute-start | bytes 786440 | tf_op jit(solution)/shard_map/ppermute | solution.py:31
  160.8 1.8 %collective-permute-done.2 = bf16[2,16,16,256]{3,2,1,0:T(8,128)(2,1)S(1)} collective-permute-done((bf16[2,16,16,256]{3,2,1,0:T(8,128)(2,1)S(1)}, bf16[2,16,16,256]{3,2,1,0:T(8,128)(2,1)S(1)}, u32[]{:S(2)}, u32[]{:S(2)}) %collective-permute-start.2) | collective-permute-done | bytes 262176 | tf_op jit(solution)/shard_map/ppermute | solution.py:31
  162.7 3.9 %collective-permute-done.3 = bf16[2,16,16,256]{3,2,1,0:T(8,128)(2,1)S(1)} collective-permute-done((bf16[2,16,16,256]{3,2,1,0:T(8,128)(2,1)S(1)}, bf16[2,16,16,256]{3,2,1,0:T(8,128)(2,1)S(1)}, u32[]{:S(2)}, u32[]{:S(2)}) %collective-permute-start.3) | collective-permute-done | bytes 262176 | tf_op jit(solution)/shard_map/ppermute | solution.py:31
  166.7 2.3 %multiply_subtract_fusion = f32[8,16,16,256]{3,2,1,0:T(8,128)} fusion(f32[8,16,16,256]{3,2,1,0:T(8,128)S(1)} %fusion.18, f32[8,16,16,256]{3,2,1,0:T(8,128)S(1)} %copy.52, bf16[8,16,16,256]{3,2,1,0:T(8,128)(2,1)S(1)} %copy-done.2, f32[8,16,256]{2,1,0:T(8,128)S(1)} %copy-done.3, s32[8,16,256]{2,1,0:T(8,128)S(1)} %copy-done.4, f32[]{:T(128)} %bitcast.1, ...), kind=kLoop, calls=%fused_computation.20 | loop fusion | flops 5767168 | bytes 7635016 | tf_op jit(solution)/shard_map/sub | solution.py:92
  (34 shorter events, 7.1 us)
Async XLA Ops:
  0.0 25.8 %copy-start = (bf16[128,80,3,3]{0,1,3,2:T(8,128)(2,1)S(1)}, bf16[128,80,3,3]{0,1,3,2:T(8,128)(2,1)}, u32[]{:S(2)}) copy-start(bf16[128,80,3,3]{0,1,3,2:T(8,128)(2,1)} %param.28) | copy-start | bytes 552964
  0.0 8.9 %copy-start.5 = (s32[8,16,256]{2,1,0:T(8,128)S(1)}, s32[8,16,256]{2,1,0:T(8,128)}, u32[]{:S(2)}) copy-start(s32[8,16,256]{2,1,0:T(8,128)} %param.25) | copy-start | bytes 393220
  2.2 10.2 %copy-start.2 = (bf16[8,16,16,256]{3,2,1,0:T(8,128)(2,1)S(1)}, bf16[8,16,16,256]{3,2,1,0:T(8,128)(2,1)}, u32[]{:S(2)}) copy-start(bf16[8,16,16,256]{3,2,1,0:T(8,128)(2,1)} %param.23) | copy-start | bytes 3145732
  2.3 7.9 %collective-permute-start = (bf16[2,16,16,256]{3,2,1,0:T(8,128)(2,1)S(1)}, bf16[2,16,16,256]{3,2,1,0:T(8,128)(2,1)S(1)}, u32[]{:S(2)}, u32[]{:S(2)}) collective-permute-start(bf16[2,16,16,256]{3,2,1,0:T(8,128)(2,1)S(1)} %get-tuple-element.90), channel_id=1, source_target_pairs={{0,1},{1,2},{2,3},{3,4},{4,5},{5,6},{6,7},{7,8},{8,9},{9,10},{10,1... | collective-permute-start | bytes 786440 | tf_op jit(solution)/shard_map/ppermute | solution.py:22
  6.9 7.7 %collective-permute-start.1 = (bf16[2,16,16,256]{3,2,1,0:T(8,128)(2,1)S(1)}, bf16[2,16,16,256]{3,2,1,0:T(8,128)(2,1)S(1)}, u32[]{:S(2)}, u32[]{:S(2)}) collective-permute-start(bf16[2,16,16,256]{3,2,1,0:T(8,128)(2,1)S(1)} %get-tuple-element.89), channel_id=1, source_target_pairs={{1,0},{2,1},{3,2},{4,3},{5,4},{6,5},{7,6},{8,7},{9,8},{10,9},{11,1... | collective-permute-start | bytes 786440 | tf_op jit(solution)/shard_map/ppermute | solution.py:23
  25.8 29.5 %copy-start.7 = (bf16[16,128,3,3]{1,0,3,2:T(8,128)(2,1)S(1)}, bf16[16,128,3,3]{1,0,3,2:T(8,128)(2,1)}, u32[]{:S(2)}) copy-start(bf16[16,128,3,3]{1,0,3,2:T(8,128)(2,1)} %param.30) | copy-start | bytes 110596
  25.8 29.5 %copy-start.8 = (f32[128]{0:T(128)S(1)}, f32[128]{0:T(128)}, u32[]{:S(2)}) copy-start(f32[128]{0:T(128)} %param.29) | copy-start | bytes 1540
  49.6 5.7 %copy-start.9 = (f32[8,128,16,256]{1,0,3,2:T(8,128)}, f32[8,128,16,256]{1,0,3,2:T(8,128)S(1)}, u32[]{:S(2)}) copy-start(f32[8,128,16,256]{1,0,3,2:T(8,128)S(1)} %fusion.22) | copy-start | bytes 50331652
  77.7 8.3 %copy-start.3 = (f32[8,16,256]{2,1,0:T(8,128)S(1)}, f32[8,16,256]{2,1,0:T(8,128)}, u32[]{:S(2)}) copy-start(f32[8,16,256]{2,1,0:T(8,128)} %param.24) | copy-start | bytes 393220
  77.7 8.3 %copy-start.6 = (f32[16]{0:T(128)S(1)}, f32[16]{0:T(128)}, u32[]{:S(2)}) copy-start(f32[16]{0:T(128)} %param.31) | copy-start | bytes 196
  148.3 4.6 %copy-start.1 = (f32[8,80,16,256]{3,2,1,0:T(8,128)S(1)}, f32[8,80,16,256]{3,2,1,0:T(8,128)}, u32[]{:S(2)}) copy-start(f32[8,80,16,256]{3,2,1,0:T(8,128)} %copy.54) | copy-start | bytes 31457284
  154.9 7.7 %collective-permute-start.2 = (bf16[2,16,16,256]{3,2,1,0:T(8,128)(2,1)S(1)}, bf16[2,16,16,256]{3,2,1,0:T(8,128)(2,1)S(1)}, u32[]{:S(2)}, u32[]{:S(2)}) collective-permute-start(bf16[2,16,16,256]{3,2,1,0:T(8,128)(2,1)S(1)} %slice.338), channel_id=1, source_target_pairs={{1,0},{2,1},{3,2},{4,3},{5,4},{6,5},{7,6},{8,7},{9,8},{10,9},{11,1... | collective-permute-start | bytes 786440 | tf_op jit(solution)/shard_map/ppermute | solution.py:31
  156.9 9.7 %collective-permute-start.3 = (bf16[2,16,16,256]{3,2,1,0:T(8,128)(2,1)S(1)}, bf16[2,16,16,256]{3,2,1,0:T(8,128)(2,1)S(1)}, u32[]{:S(2)}, u32[]{:S(2)}) collective-permute-start(bf16[2,16,16,256]{3,2,1,0:T(8,128)(2,1)S(1)} %slice.337), channel_id=1, source_target_pairs={{0,1},{1,2},{2,3},{3,4},{4,5},{5,6},{6,7},{7,8},{8,9},{9,10},{10,1... | collective-permute-start | bytes 786440 | tf_op jit(solution)/shard_map/ppermute | solution.py:31
  160.6 6.1 %copy-start.4 = (s32[8,16,256]{2,1,0:T(8,128)S(1)}, s32[8,16,256]{2,1,0:T(8,128)}, u32[]{:S(2)}) copy-start(s32[8,16,256]{2,1,0:T(8,128)} %param.26) | copy-start | bytes 393220
where the time goes:
time: 172 us; the launch traced here: 169 us
  matrix products  84.9 us (49%)
  local copies, waits for them, and re-layouts  46.8 us (27%)
  other arithmetic  16.2 us (9%)
  starting transfers between devices  12.1 us (7%)
  waiting for transfers between devices  8.02 us (5%)
    conv_general_dilated x4, matrix products, conv(): lax.conv_general_dilated(value, kernel, (1, 1), ((1, 1), (1, 1)), dimensi...  84.9 us
    conv_general_dilated x2, local copies, waits for them, and re-layouts, conv(): lax.conv_general_dilated(value, kernel, (1, 1), ((1, 1), (1, 1)), dimensi...  20 us
    concatenate x1, local copies, waits for them, and re-layouts, stack_windows(): return jnp.concatenate([source[k:k + frames] for k in range(span)], axis=1)  8.99 us
    unnamed x20, local copies, waits for them, and re-layouts  7.68 us
    convert_element_type x1, local copies, waits for them, and re-layouts, per_device(): misfit_b = misfit.astype(jnp.bfloat16)  7.46 us
    ppermute x2, waiting for transfers between devices, passed_along(): lax.ppermute(value, axis, [(source, source + steps) for source in range(i...  5.72 us
    ppermute x2, starting transfers between devices, passed_along(): lax.ppermute(value, axis, [(source, source + steps) for source in range(i...  5.56 us
    ppermute x1, starting transfers between devices, with_halo(): before = lax.ppermute(last, axis, up)  4.64 us
  transfers between devices with their start and end apart: 4, of which 4 were waited for; matrix products, arithmetic and copies ran while one was open for 2% of the time, Pallas kernels for 0%

commit v1 on v0

v1 whole, which is shorter than its diff:
```python
import functools

import jax
import jax.numpy as jnp
from jax import lax
from jax.experimental import pallas as pl
from jax.experimental.pallas import tpu as pltpu
from jax.sharding import PartitionSpec as P

STEPS = 64
sigma_low = 0.1
sigma_ratio = 20.0
F32 = jnp.float32
BF16 = jnp.bfloat16


def shifted(x, by):
    lanes = x.shape[1]
    lane = lax.broadcasted_iota(jnp.int32, x.shape, 1)
    edge = 0 if by > 0 else lanes - 1
    return jnp.where(lane == edge, 0.0, pltpu.roll(x, by % lanes, 1))


def main_kernel(
    dims,
    cw,
    b2s,
    noisy,
    before,
    after,
    obs,
    mask,
    chan,
    wf,
    b1,
    ws,
    out,
    sent,
    w1,
    w2t,
    wt1,
    wide,
    nperm,
    deriv,
    part,
    codes,
    mis,
    grads,
    qs,
    rest,
    stage,
):
    frames, chans, rows, cols, hid, span = dims
    half = span // 2
    taps = 9 * chans
    c_in, weight = cw[0], cw[1]
    dot = functools.partial(jnp.dot, preferred_element_type=F32)

    blocks = []
    for k in range(span):
        for ab in range(9):
            blocks.append(wf[ab * span * chans + k * chans : ab * span * chans + (k + 1) * chans, :])
    bias = b1[...]
    high = bias.astype(BF16)
    left = bias - high.astype(F32)
    mid = left.astype(BF16)
    low = (left - mid.astype(F32)).astype(BF16)
    depth = w1.shape[1]
    tail = depth - span * taps
    sub = lax.broadcasted_iota(jnp.int32, (tail, hid), 0)
    extra = jnp.where(
        sub == 0,
        high.astype(F32),
        jnp.where(sub == 1, mid.astype(F32), jnp.where(sub == 2, low.astype(F32), 0.0)),
    )
    blocks.append(extra.astype(BF16))
    stacked = jnp.concatenate(blocks, axis=0).astype(F32) * 0.5
    w1[...] = stacked.T.astype(BF16)
    w2t[...] = (ws[...].astype(F32) * 0.5).T.astype(BF16)
    for sp in range(2):
        for ab in range(9):
            for tp in range(span + 1):
                k = sp - tp + 2 * half
                at = (sp * 9 + ab) * chans
                if 0 <= k < span:
                    piece = wf[ab * span * chans + k * chans : ab * span * chans + (k + 1) * chans, :]
                else:
                    piece = jnp.zeros((chans, hid), BF16)
                wt1[at : at + chans, tp * hid : (tp + 1) * hid] = piece

    row_c = lax.broadcasted_iota(jnp.int32, (chans, cols), 0)
    b2 = jnp.zeros((chans, cols), F32)
    for c in range(chans):
        b2 = jnp.where(row_c == c, b2s[c], b2)

    size = chans * rows
    i0 = lax.broadcasted_iota(jnp.int32, (size, size), 0)
    i1 = lax.broadcasted_iota(jnp.int32, (size, size), 1)
    perm = jnp.where(
        (i0 % chans) * rows + i0 // chans == i1, 1.0, 0.0
    ).astype(BF16)
    zero48 = jnp.zeros((3 * chans, cols), BF16)

    def spread(x, slot):
        scaled = (c_in * x).astype(BF16).astype(F32)
        shifts = [shifted(scaled, 1).astype(BF16), scaled.astype(BF16), shifted(scaled, -1).astype(BF16)]
        wide[slot, 0 : 3 * chans, :] = zero48
        wide[slot, (rows + 1) * 3 * chans :, :] = zero48
        for y in range(rows):
            for b in range(3):
                at = (y + 1) * 3 * chans + b * chans
                wide[slot, at : at + chans, :] = shifts[b][y * chans : (y + 1) * chans, :]

    for f in range(half):
        spread(dot(perm, before[f]), f)
        spread(dot(perm, after[f]), half + frames + f)

    def prepare(f, carry):
        x = dot(perm, noisy[f])
        nperm[f] = x.astype(BF16)
        spread(x, half + f)
        return carry

    lax.fori_loop(0, frames, prepare, 0)

    sub = lax.broadcasted_iota(jnp.int32, (tail, cols), 0)
    ones = jnp.where(sub < 3, 1.0, 0.0).astype(BF16)
    zero_g = jnp.zeros((hid, cols), BF16)
    for f in range(half):
        for y in range(rows):
            grads[f, y] = zero_g
            grads[half + frames + f, y] = zero_g
    mis[0] = zero48
    mis[rows + 1] = zero48

    def forward(f, carry):
        codes[...] = jnp.where(mask[f] == 1, chan[f], -1)

        def hidden_row(r):
            pieces = [wide[f + k, r * 3 * chans : (r + 3) * 3 * chans, :] for k in range(span)]
            h = dot(w1[...], jnp.concatenate(pieces + [ones], axis=0))
            u = 1.0 + jnp.tanh(h)
            act = h * u
            deriv[r] = u * (1.0 + (h + h) - act)
            part[r] = dot(ws[...], act.astype(BF16))

        def misfit_row(y):
            total = None
            for a in range(3):
                r = y + a - 1
                if 0 <= r < rows:
                    term = part[r, a * 3 * chans : (a + 1) * 3 * chans, :]
                    total = term if total is None else total + term
            second = (
                shifted(total[:chans], 1) + total[chans : 2 * chans] + shifted(total[2 * chans :], -1)
            )
            den = nperm[f, y * chans : (y + 1) * chans, :].astype(F32) + second + b2
            code = codes[y : y + 1, :]
            miss = jnp.where(row_c == code, den - obs[f, y : y + 1, :], 0.0)
            rest[f, y * chans : (y + 1) * chans, :] = den - weight * miss
            mis[y + 1, :chans, :] = shifted(miss, -1).astype(BF16)
            mis[y + 1, chans : 2 * chans, :] = miss.astype(BF16)
            mis[y + 1, 2 * chans :, :] = shifted(miss, 1).astype(BF16)

        def grad_row(y):
            v = jnp.concatenate([mis[y + 2], mis[y + 1], mis[y]], axis=0)
            grads[f + half, y] = (dot(w2t[...], v) * deriv[y]).astype(BF16)

        for step in range(rows + 2):
            if step < rows:
                hidden_row(step)
            if 1 <= step <= rows:
                misfit_row(step - 1)
            if step >= 2:
                grad_row(step - 2)
        return carry

    lax.fori_loop(0, frames, forward, 0)

    def put(sp, y, value):
        for j in range(cols // 128):
            stage[sp, j, pl.ds(y, chans, stride=rows), :] = value[:, j * 128 : (j + 1) * 128]

    def back_rows(slots, w, emit):
        def q_row(r):
            v = jnp.concatenate([grads[s, r] for s in slots], axis=0)
            qs[r] = dot(w, v)

        def out_row(y):
            for sp in range(2):
                total = None
                for a in range(3):
                    r = y - a + 1
                    if 0 <= r < rows:
                        at = (sp * 9 + a * 3) * chans
                        term = qs[r, at : at + 3 * chans, :]
                        total = term if total is None else total + term
                back = (
                    shifted(total[:chans], -1)
                    + total[chans : 2 * chans]
                    + shifted(total[2 * chans :], 1)
                )
                emit(sp, y, back)

        for step in range(rows + 1):
            if step < rows:
                q_row(step)
            if step >= 1:
                out_row(step - 1)

    def pair(p, carry):
        s0 = 2 * p

        def emit(sp, y, back):
            own = rest[s0 + sp, y * chans : (y + 1) * chans, :]
            put(sp, y, own - (weight * c_in) * back)

        back_rows([s0 + j for j in range(span + 1)], wt1[...], emit)
        for sp in range(2):
            for j in range(cols // 128):
                out[s0 + sp, :, j * 128 : (j + 1) * 128] = stage[sp, j]
        return carry

    lax.fori_loop(0, frames // 2, pair, 0)

    for side in range(2):
        first = half if side == 0 else frames
        lanes = (span - 1) * hid if side == 0 else 0
        back_rows([first, first + 1], wt1[:, lanes : lanes + 2 * hid], put)
        for sp in range(2):
            for j in range(cols // 128):
                sent[2 * side + sp, :, j * 128 : (j + 1) * 128] = stage[sp, j].astype(BF16)


def per_device(noisy, observed, obs_mask, obs_channel, step_index, w_first, b_first, w_second, b_second):
    frames, chans, rows, cols = noisy.shape
    hid = w_first.shape[0]
    span = w_first.shape[1] // chans
    half = span // 2
    size = chans * rows
    count = lax.axis_size("tm")
    up = [(i, i + 1) for i in range(count - 1)]
    down = [(i + 1, i) for i in range(count - 1)]

    level = step_index[0].astype(F32) / F32(STEPS - 1)
    sigma = F32(sigma_low) * jnp.exp(jnp.log(F32(sigma_ratio)) * level)
    c_in = 1.0 / jnp.sqrt(1.0 + sigma * sigma)
    weight = 1.0 / (1.0 + sigma * sigma)
    cw = jnp.stack([c_in, weight])

    flat = noisy.reshape(frames, size, cols)
    before = lax.ppermute(flat[frames - half :], "tm", up)
    after = lax.ppermute(flat[:half], "tm", down)

    depth = -(-span * 9 * chans // 256) * 256
    dims = (frames, chans, rows, cols, hid, span)
    vmem = pl.BlockSpec(memory_space=pltpu.VMEM)
    smem = pl.BlockSpec(memory_space=pltpu.SMEM)
    out, sent = pl.pallas_call(
        functools.partial(main_kernel, dims),
        out_shape=(
            jax.ShapeDtypeStruct((frames, size, cols), F32),
            jax.ShapeDtypeStruct((2 * half, size, cols), BF16),
        ),
        in_specs=[smem, smem] + [vmem] * 9,
        out_specs=(vmem, vmem),
        scratch_shapes=[
            pltpu.VMEM((hid, depth), BF16),
            pltpu.VMEM((hid, 9 * chans), BF16),
            pltpu.VMEM((18 * chans, (span + 1) * hid), BF16),
            pltpu.VMEM((frames + 2 * half, (rows + 2) * 3 * chans, cols), BF16),
            pltpu.VMEM((frames, size, cols), BF16),
            pltpu.VMEM((rows, hid, cols), F32),
            pltpu.VMEM((rows, 9 * chans, cols), F32),
            pltpu.VMEM((rows, cols), jnp.int32),
            pltpu.VMEM((rows + 2, 3 * chans, cols), BF16),
            pltpu.VMEM((frames + 2 * half, rows, hid, cols), BF16),
            pltpu.VMEM((rows, 18 * chans, cols), F32),
            pltpu.VMEM((frames, size, cols), F32),
            pltpu.VMEM((2, cols // 128, size, 128), F32),
        ],
        compiler_params=pltpu.CompilerParams(vmem_limit_bytes=56 << 20),
    )(
        cw,
        b_second,
        flat,
        before,
        after,
        observed,
        obs_mask,
        obs_channel,
        jnp.transpose(w_first, (2, 3, 1, 0)).reshape(9 * span * chans, hid),
        b_first.reshape(1, hid),
        jnp.transpose(w_second, (2, 3, 0, 1)).reshape(9 * chans, hid),
    )
    from_right = lax.ppermute(sent[:half], "tm", down).astype(F32)
    from_left = lax.ppermute(sent[half:], "tm", up).astype(F32)
    out = out.at[frames - half :].add(-(weight * c_in) * from_right)
    out = out.at[:half].add(-(weight * c_in) * from_left)
    return out.reshape(frames, chans, rows, cols)


def solution(mesh):
    return jax.shard_map(
        per_device,
        mesh=mesh,
        in_specs=(
            P(("groups", "tm"), None, None, None),
            P(("groups", "tm"), None, None),
            P(("groups", "tm"), None, None),
            P(("groups", "tm"), None, None),
            P("groups"),
            P(),
            P(),
            P(),
            P(),
        ),
        out_specs=P(("groups", "tm"), None, None, None),
        check_vma=False,
    )
```

time: 172 us -> 103 us (0.60); the launches traced: 169 us -> 103 us
  matrix products: 84.9 us -> 0 us
  Pallas kernels: 0 us -> 74 us
  local copies, waits for them, and re-layouts: 46.8 us -> 2.83 us
  other arithmetic: 16.2 us -> 4.38 us
    conv_general_dilated x4 -> x0, matrix products: 84.9 us -> none  [conv(): lax.conv_general_dilated(value, kernel, (1, 1), ((1, 1), (1, 1)), dimensi...]
    pallas_call x0 -> x1, Pallas kernels: none -> 74 us  [per_device(): pl.pallas_call(functools.partial(main_kernel, dims), out_shape=(jax.Shape...]
    conv_general_dilated x2 -> x0, local copies, waits for them, and re-layouts: 20 us -> none  [conv(): lax.conv_general_dilated(value, kernel, (1, 1), ((1, 1), (1, 1)), dimensi...]
    concatenate x1 -> x0, local copies, waits for them, and re-layouts: 8.99 us -> none  [stack_windows(): return jnp.concatenate([source[k:k + frames] for k in range(span)], axis=1)]
    convert_element_type x1 -> x0, local copies, waits for them, and re-layouts: 7.46 us -> none  [per_device(): misfit_b = misfit.astype(jnp.bfloat16)]
    unnamed x20 -> x4, local copies, waits for them, and re-layouts: 7.68 us -> 0.7 us
    unnamed x4 -> x0, other arithmetic: 4.49 us -> none
    convert_element_type x2 -> x0, other arithmetic: 4.03 us -> none  [the longest x1 2.6 us: per_device(): misfit_b = misfit.astype(jnp.bfloat16)]
  transfers between devices with their start and end apart: 4 -> 4, of which waited for: 4 -> 3; matrix products, arithmetic and copies ran while one was open for 2% -> 2% of each run, Pallas kernels for 0% -> 0%
where the time goes in v1:
time: 103 us
  Pallas kernels  74 us (72%)
  starting transfers between devices  12 us (12%)
  waiting for transfers between devices  8.57 us (8%)
  other arithmetic  4.38 us (4%)
  local copies, waits for them, and re-layouts  2.83 us (3%)
    pallas_call x1, Pallas kernels, per_device(): pl.pallas_call(functools.partial(main_kernel, dims), out_shape=(jax.Shape...  74 us
    ppermute x1, starting transfers between devices, per_device(): before = lax.ppermute(flat[frames - half:], 'tm', up)  4.51 us
    ppermute x1, waiting for transfers between devices, per_device(): after = lax.ppermute(flat[:half], 'tm', down)  4.38 us
    ppermute x1, starting transfers between devices, per_device(): from_left = lax.ppermute(sent[half:], 'tm', up).astype(F32)  3.64 us
    ppermute x1, waiting for transfers between devices, per_device(): from_right = lax.ppermute(sent[:half], 'tm', down).astype(F32)  2.11 us
    ppermute x1, waiting for transfers between devices, per_device(): from_left = lax.ppermute(sent[half:], 'tm', up).astype(F32)  2.08 us
  transfers between devices with their start and end apart: 4, of which 3 were waited for; matrix products, arithmetic and copies ran while one was open for 2% of the time, Pallas kernels for 0%

profile of v1, /device:TPU:1, one launch (start us, length us, event | category | flops | bytes accessed | tf_op | source)
XLA Modules:
  0.0 102.6 jit_solution(11361309929159304715)
XLA Ops:
  0.0 1.1 %fusion.1 = (bf16[2,16,16,256]{3,2,1,0:T(8,128)(2,1)S(1)}, bf16[2,16,16,256]{3,2,1,0:T(8,128)(2,1)S(1)}) fusion(bf16[8,16,16,256]{3,2,1,0:T(8,128)(2,1)} %param.13), kind=kLoop, calls=%fused_computation.4 | loop fusion | bytes 1048576 | tf_op jit(solution)/shard_map/slice | solution.py:253
  1.1 4.5 %collective-permute-start = (bf16[2,256,256]{2,1,0:T(8,128)(2,1)S(1)}, bf16[2,256,256]{2,1,0:T(8,128)(2,1)S(1)}, u32[]{:S(2)}, u32[]{:S(2)}) collective-permute-start(bf16[2,256,256]{2,1,0:T(8,128)(2,1)S(1)} %bitcast.14), channel_id=1, source_target_pairs={{0,1},{1,2},{2,3},{3,4},{4,5},{5,6},{6,7},{7,8},{8,9},{9,10},{10,1... | collective-permute-start | bytes 786440 | tf_op jit(solution)/shard_map/ppermute | solution.py:252
  5.6 1.9 %collective-permute-start.1 = (bf16[2,256,256]{2,1,0:T(8,128)(2,1)S(1)}, bf16[2,256,256]{2,1,0:T(8,128)(2,1)S(1)}, u32[]{:S(2)}, u32[]{:S(2)}) collective-permute-start(bf16[2,256,256]{2,1,0:T(8,128)(2,1)S(1)} %bitcast.13), channel_id=1, source_target_pairs={{1,0},{2,1},{3,2},{4,3},{5,4},{6,5},{7,6},{8,7},{9,8},{10,9},{11,1... | collective-permute-start | bytes 786440 | tf_op jit(solution)/shard_map/ppermute | solution.py:253
  8.3 0.6 pad_maximum_fusion.cw
  8.9 0.0 collective-permute-done.before
  8.9 0.0 copy-start
  8.9 4.4 %collective-permute-done.1.after = bf16[2,256,256]{2,1,0:T(8,128)(2,1)S(1)} collective-permute-done((bf16[2,256,256]{2,1,0:T(8,128)(2,1)S(1)}, bf16[2,256,256]{2,1,0:T(8,128)(2,1)S(1)}, u32[]{:S(2)}, u32[]{:S(2)}) %collective-permute-start.1) | collective-permute-done | bytes 262176 | tf_op jit(solution)/shard_map/ppermute | solution.py:253
  13.3 0.0 copy-start.1
  13.3 0.0 copy-done
  13.3 0.7 copy-done.1
  14.0 74.0 %shard_map.91 = (f32[8,256,256]{2,1,0:T(8,128)}, bf16[4,256,256]{2,1,0:T(8,128)(2,1)}) custom-call(f32[2]{0:T(128)} %pad_maximum_fusion.cw, f32[16]{0:T(128)} %b2s.1, bf16[8,256,256]{2,1,0:T(8,128)(2,1)} %bitcast.12, bf16[2,256,256]{2,1,0:T(8,128)(2,1)} %copy-done, bf16[2,256,256]{2,1,0:T(8,128)(2,1)} %copy-done.1, f32[8,16,256]{2,1,0:T(8,128)} %obs.1, ...), custom_call_target="tpu_custom_call" | custom-call | tf_op jit(solution)/shard_map/pallas_call | solution.py:259
  88.0 1.1 %fusion.2 = (bf16[2,256,256]{2,1,0:T(8,128)(2,1)S(1)}, bf16[2,256,256]{2,1,0:T(8,128)(2,1)S(1)}) fusion(bf16[4,256,256]{2,1,0:T(8,128)(2,1)} %get-tuple-element.32), kind=kLoop, calls=%fused_computation.5 | loop fusion | bytes 1048576 | tf_op jit(solution)/shard_map/slice | solution.py:297
  89.1 1.9 %collective-permute-start.2 = (bf16[2,256,256]{2,1,0:T(8,128)(2,1)S(1)}, bf16[2,256,256]{2,1,0:T(8,128)(2,1)S(1)}, u32[]{:S(2)}, u32[]{:S(2)}) collective-permute-start(bf16[2,256,256]{2,1,0:T(8,128)(2,1)S(1)} %get-tuple-element.36), channel_id=1, source_target_pairs={{1,0},{2,1},{3,2},{4,3},{5,4},{6,5},{7,6},{8,7},{9,8},{10,9},{11,1... | collective-permute-start | bytes 786440 | tf_op jit(solution)/shard_map/ppermute | solution.py:296
  91.0 3.6 %collective-permute-start.3 = (bf16[2,256,256]{2,1,0:T(8,128)(2,1)S(1)}, bf16[2,256,256]{2,1,0:T(8,128)(2,1)S(1)}, u32[]{:S(2)}, u32[]{:S(2)}) collective-permute-start(bf16[2,256,256]{2,1,0:T(8,128)(2,1)S(1)} %get-tuple-element.35), channel_id=1, source_target_pairs={{0,1},{1,2},{2,3},{3,4},{4,5},{5,6},{6,7},{7,8},{8,9},{9,10},{10,1... | collective-permute-start | bytes 786440 | tf_op jit(solution)/shard_map/ppermute | solution.py:297
  94.6 2.1 %collective-permute-done.2 = bf16[2,256,256]{2,1,0:T(8,128)(2,1)S(1)} collective-permute-done((bf16[2,256,256]{2,1,0:T(8,128)(2,1)S(1)}, bf16[2,256,256]{2,1,0:T(8,128)(2,1)S(1)}, u32[]{:S(2)}, u32[]{:S(2)}) %collective-permute-start.2) | collective-permute-done | bytes 262176 | tf_op jit(solution)/shard_map/ppermute | solution.py:296
  96.8 1.9 %add_dynamic-update-slice_fusion = f32[8,256,256]{2,1,0:T(8,128)} fusion(f32[8,256,256]{2,1,0:T(8,128)} %get-tuple-element.31, bf16[2,256,256]{2,1,0:T(8,128)(2,1)S(1)} %collective-permute-done.2, f32[]{:T(128)} %bitcast.8), kind=kLoop, calls=%fused_computation.2 | loop fusion | flops 393216 | bytes 1311232 | tf_op jit(solution)/shard_map/scatter-add | solution.py:298
  98.6 2.1 %collective-permute-done.3 = bf16[2,256,256]{2,1,0:T(8,128)(2,1)S(1)} collective-permute-done((bf16[2,256,256]{2,1,0:T(8,128)(2,1)S(1)}, bf16[2,256,256]{2,1,0:T(8,128)(2,1)S(1)}, u32[]{:S(2)}, u32[]{:S(2)}) %collective-permute-start.3) | collective-permute-done | bytes 262176 | tf_op jit(solution)/shard_map/ppermute | solution.py:297
  100.7 1.9 %fusion = f32[8,256,256]{2,1,0:T(8,128)} fusion(f32[8,256,256]{2,1,0:T(8,128)} %add_dynamic-update-slice_fusion, bf16[2,256,256]{2,1,0:T(8,128)(2,1)S(1)} %collective-permute-done.3, f32[]{:T(128)} %bitcast.8), kind=kLoop, calls=%fused_computation.1 | loop fusion | flops 393216 | bytes 1311232 | tf_op jit(solution)/shard_map/scatter-add | solution.py:299
Async XLA Ops:
  1.1 7.8 %collective-permute-start = (bf16[2,256,256]{2,1,0:T(8,128)(2,1)S(1)}, bf16[2,256,256]{2,1,0:T(8,128)(2,1)S(1)}, u32[]{:S(2)}, u32[]{:S(2)}) collective-permute-start(bf16[2,256,256]{2,1,0:T(8,128)(2,1)S(1)} %bitcast.14), channel_id=1, source_target_pairs={{0,1},{1,2},{2,3},{3,4},{4,5},{5,6},{6,7},{7,8},{8,9},{9,10},{10,1... | collective-permute-start | bytes 786440 | tf_op jit(solution)/shard_map/ppermute | solution.py:252
  5.6 7.7 %collective-permute-start.1 = (bf16[2,256,256]{2,1,0:T(8,128)(2,1)S(1)}, bf16[2,256,256]{2,1,0:T(8,128)(2,1)S(1)}, u32[]{:S(2)}, u32[]{:S(2)}) collective-permute-start(bf16[2,256,256]{2,1,0:T(8,128)(2,1)S(1)} %bitcast.13), channel_id=1, source_target_pairs={{1,0},{2,1},{3,2},{4,3},{5,4},{6,5},{7,6},{8,7},{9,8},{10,9},{11,1... | collective-permute-start | bytes 786440 | tf_op jit(solution)/shard_map/ppermute | solution.py:253
  8.9 4.4 %copy-start = (bf16[2,256,256]{2,1,0:T(8,128)(2,1)}, bf16[2,256,256]{2,1,0:T(8,128)(2,1)S(1)}, u32[]{:S(2)}) copy-start(bf16[2,256,256]{2,1,0:T(8,128)(2,1)S(1)} %collective-permute-done.before) | copy-start | bytes 786436
  13.3 0.7 copy-start.1
  89.1 7.7 %collective-permute-start.2 = (bf16[2,256,256]{2,1,0:T(8,128)(2,1)S(1)}, bf16[2,256,256]{2,1,0:T(8,128)(2,1)S(1)}, u32[]{:S(2)}, u32[]{:S(2)}) collective-permute-start(bf16[2,256,256]{2,1,0:T(8,128)(2,1)S(1)} %get-tuple-element.36), channel_id=1, source_target_pairs={{1,0},{2,1},{3,2},{4,3},{5,4},{6,5},{7,6},{8,7},{9,8},{10,9},{11,1... | collective-permute-start | bytes 786440 | tf_op jit(solution)/shard_map/ppermute | solution.py:296
  91.0 9.7 %collective-permute-start.3 = (bf16[2,256,256]{2,1,0:T(8,128)(2,1)S(1)}, bf16[2,256,256]{2,1,0:T(8,128)(2,1)S(1)}, u32[]{:S(2)}, u32[]{:S(2)}) collective-permute-start(bf16[2,256,256]{2,1,0:T(8,128)(2,1)S(1)} %get-tuple-element.35), channel_id=1, source_target_pairs={{0,1},{1,2},{2,3},{3,4},{4,5},{5,6},{6,7},{7,8},{8,9},{9,10},{10,1... | collective-permute-start | bytes 786440 | tf_op jit(solution)/shard_map/ppermute | solution.py:297

commit v2 on v1

v2 whole, which is shorter than its diff:
```python
import functools

import jax
import jax.numpy as jnp
from jax import lax
from jax.experimental import pallas as pl
from jax.experimental.pallas import tpu as pltpu
from jax.sharding import PartitionSpec as P

STEPS = 64
sigma_low = 0.1
sigma_ratio = 20.0
F32 = jnp.float32
BF16 = jnp.bfloat16


def shifted(x, by):
    lanes = x.shape[1]
    lane = lax.broadcasted_iota(jnp.int32, x.shape, 1)
    edge = 0 if by > 0 else lanes - 1
    return jnp.where(lane == edge, 0.0, pltpu.roll(x, by % lanes, 1))


class Unit:

    def __init__(self, index):
        self.index = index
        self.turn = 0

    def product(self, sums, left, right):
        slot = self.turn
        self.turn = 1 - slot
        pltpu.matmul_push_rhs(right, slot, self.index)
        at = 0
        for n, total in enumerate(sums):
            size = total.shape[0]
            pltpu.matmul_acc_lhs(
                total, left[at : at + size, :], load_staged_rhs=slot if n == 0 else None
            )
            at += size


def main_kernel(
    dims,
    cw,
    b2s,
    noisy,
    before,
    after,
    obs,
    mask,
    chan,
    wf,
    b1,
    ws,
    out,
    sent,
    w1,
    w2,
    w2t,
    wt1,
    wide,
    nperm,
    deriv,
    part,
    acts,
    mis,
    grads,
    qs,
    rest,
    stage,
):
    frames, chans, rows, cols, hid, span = dims
    half = span // 2
    taps = 9 * chans
    group = 3 * chans
    pairs = rows // 2
    c_in, weight = cw[0], cw[1]
    units = (Unit(0), Unit(1))

    def first_block(k, ab):
        at = (ab * span + k) * chans
        return wf[at : at + chans, :]

    blocks = [first_block(k, ab) for k in range(span) for ab in range(9)]
    bias = b1[...]
    high = bias.astype(BF16)
    left = bias - high.astype(F32)
    mid = left.astype(BF16)
    low = (left - mid.astype(F32)).astype(BF16)
    depth = w1.shape[1]
    tail = depth - span * taps
    sub = lax.broadcasted_iota(jnp.int32, (tail, hid), 0)
    extra = jnp.where(
        sub == 0,
        high.astype(F32),
        jnp.where(sub == 1, mid.astype(F32), jnp.where(sub == 2, low.astype(F32), 0.0)),
    )
    blocks.append(extra.astype(BF16))
    stacked = jnp.concatenate(blocks, axis=0).astype(F32) * 0.5
    w1[...] = stacked.T.astype(BF16)
    second = ws[...]
    zero_group = jnp.zeros((group, hid), BF16)

    def second_block(a):
        return second[a * group : (a + 1) * group, :] if 0 <= a < 3 else zero_group

    for o in range(4):
        for i in range(2):
            w2[o * group : (o + 1) * group, i * hid : (i + 1) * hid] = second_block(i + 2 - o)
    for i in range(2):
        tall = [second_block(i + 2 - m) for m in range(4)]
        tall.append(jnp.zeros((2 * hid - 4 * group, hid), BF16))
        tall = jnp.concatenate(tall, axis=0).astype(F32) * 0.5
        w2t[i * hid : (i + 1) * hid, :] = tall.T.astype(BF16)
    for sp in range(2):
        for ab in range(9):
            for tp in range(span + 1):
                k = sp - tp + 2 * half
                at = (sp * 9 + ab) * chans
                piece = first_block(k, ab) if 0 <= k < span else jnp.zeros((chans, hid), BF16)
                wt1[at : at + chans, tp * hid : (tp + 1) * hid] = piece

    row_c = lax.broadcasted_iota(jnp.int32, (chans, cols), 0)
    b2 = jnp.zeros((chans, cols), F32)
    for c in range(chans):
        b2 = jnp.where(row_c == c, b2s[c], b2)

    size = chans * rows
    i0 = lax.broadcasted_iota(jnp.int32, (size, size), 0)
    i1 = lax.broadcasted_iota(jnp.int32, (size, size), 1)
    perm = jnp.where((i0 % chans) * rows + i0 // chans == i1, 1.0, 0.0).astype(BF16)
    zero48 = jnp.zeros((group, cols), BF16)

    def spread(x, slot, y0):
        scaled = (c_in * x).astype(BF16).astype(F32)
        shifts = [shifted(scaled, 1).astype(BF16), scaled.astype(BF16), shifted(scaled, -1).astype(BF16)]
        for y in range(x.shape[0] // chans):
            for b in range(3):
                at = (y0 + y + 1) * group + b * chans
                wide[slot, at : at + chans, :] = shifts[b][y * chans : (y + 1) * chans, :]

    def reorder(totals):
        def frame(m, source, slot, own):
            units[m].product(totals[m], perm, source)
            wide[slot, 0:group, :] = zero48
            wide[slot, (rows + 1) * group :, :] = zero48

        def finish(m, slot, own):
            at = 0
            for total in totals[m]:
                x = matmul_pop(total)
                if own is not None:
                    nperm[own, at : at + x.shape[0], :] = x.astype(BF16)
                spread(x, slot, at // chans)
                at += x.shape[0]

        for f in range(half):
            frame(0, before[f], f, None)
            frame(1, after[f], half + frames + f, None)
            finish(0, f, None)
            finish(1, half + frames + f, None)

        def prepare(p, carry):
            for m in range(2):
                frame(m, noisy[2 * p + m], half + 2 * p + m, 2 * p + m)
            for m in range(2):
                finish(m, half + 2 * p + m, 2 * p + m)
            return carry

        lax.fori_loop(0, frames // 2, prepare, 0)

    matmul_pop = pltpu.matmul_pop
    pl.run_scoped(reorder, [[pltpu.ACC(m)((size // 4, cols), F32) for _ in range(4)] for m in range(2)])

    sub = lax.broadcasted_iota(jnp.int32, (tail, cols), 0)
    ones = jnp.where(sub < 3, 1.0, 0.0).astype(BF16)
    zero_g = jnp.zeros((hid, cols), BF16)
    for f in range(half):
        for y in range(rows):
            grads[f, y] = zero_g
            grads[half + frames + f, y] = zero_g
    mis[...] = jnp.zeros(mis.shape, BF16)

    def forward(sums1, sums2, sums3):

        def issue_first(f, t):
            for m in range(2):
                r = 2 * t + m
                pieces = [wide[f + k, r * group : (r + 3) * group, :] for k in range(span)]
                v = jnp.concatenate(pieces + [ones], axis=0)
                for k in range(depth // cols):
                    units[m].product(
                        sums1[m][t % 2], w1.at[:, k * 256 : (k + 1) * 256], v[k * 256 : (k + 1) * 256, :]
                    )

        def activate(f, t):
            for m in range(2):
                at = 0
                for total in sums1[m][t % 2]:
                    h = pltpu.matmul_pop(total)
                    u = 1.0 + jnp.tanh(h)
                    act = h * u
                    deriv[f % 2, 2 * t + m, at : at + h.shape[0], :] = u * (1.0 + (h + h) - act)
                    acts[t % 2, m * hid + at : m * hid + at + h.shape[0], :] = act.astype(BF16)
                    at += h.shape[0]

        def issue_second(t):
            units[0].product(sums2[t % 2], w2, acts[t % 2])

        def keep_second(f, t):
            for o in range(4):
                part[f % 2, t, o * group : (o + 1) * group, :] = pltpu.matmul_pop(sums2[t % 2][o])

        def misfit_row(g, y):
            t, i = y // 2, y % 2
            total = part[g % 2, t, (1 + i) * group : (2 + i) * group, :]
            other, o = (t + 1, 0) if i else (t - 1, 3)
            if 0 <= other < pairs:
                total = total + part[g % 2, other, o * group : (o + 1) * group, :]
            conv = shifted(total[:chans], 1) + total[chans : 2 * chans] + shifted(total[2 * chans :], -1)
            den = nperm[g, y * chans : (y + 1) * chans, :].astype(F32) + conv + b2
            seen = mask[g, y : y + 1, :]
            code = jnp.where(seen == 1, chan[g, y : y + 1, :], -1)
            miss = jnp.where(row_c == code, den - obs[g, y : y + 1, :], 0.0)
            rest[g, y * chans : (y + 1) * chans, :] = den - weight * miss
            at = (y + 1) * group
            mis[at : at + chans, :] = shifted(miss, -1).astype(BF16)
            mis[at + chans : at + 2 * chans, :] = miss.astype(BF16)
            mis[at + 2 * chans : at + 3 * chans, :] = shifted(miss, 1).astype(BF16)

        def issue_third(q):
            at = 2 * q * group
            units[1].product(sums3[q % 2], w2t, mis[at : at + 2 * hid, :])

        def keep_third(g, q):
            at = 0
            for total in sums3[q % 2]:
                n = total.shape[0]
                i, low = at // hid, at % hid
                y = 2 * q + i
                d = pltpu.matmul_pop(total) * deriv[g % 2, y, low : low + n, :]
                grads[g + half, y, low : low + n, :] = d.astype(BF16)
                at += n

        def body(f, g):
            for t in range(pairs + 3):
                if f is not None and 2 <= t < pairs + 2:
                    issue_second(t - 2)
                if g is not None and 2 <= t < pairs + 2:
                    issue_third(t - 2)
                if f is not None and t < pairs:
                    issue_first(f, t)
                if f is not None and 1 <= t < pairs + 1:
                    activate(f, t - 1)
                if g is not None:
                    for y in (2 * t, 2 * t + 1):
                        if y < rows:
                            misfit_row(g, y)
                if f is not None and 3 <= t < pairs + 3:
                    keep_second(f, t - 3)
                if g is not None and 3 <= t < pairs + 3:
                    keep_third(g, t - 3)

        body(0, None)

        def step(f, carry):
            body(f, f - 1)
            return carry

        lax.fori_loop(1, frames, step, 0)
        body(None, frames - 1)

    def sums(unit, size, n):
        return [[pltpu.ACC(unit)((size, cols), F32) for _ in range(n)] for _ in range(2)]

    pl.run_scoped(
        forward,
        [sums(m, hid // 2, 2) for m in range(2)],
        sums(0, group, 4),
        sums(1, hid // 2, 4),
    )

    def put(sp, y, value):
        for j in range(cols // 128):
            stage[sp, j, pl.ds(y, chans, stride=rows), :] = value[:, j * 128 : (j + 1) * 128]

    def back_rows(totals, slots, w, emit):
        def issue(t):
            for m in range(2):
                r = 2 * t + m
                for k in range(len(slots) // 2):
                    v = jnp.concatenate([grads[slots[2 * k], r], grads[slots[2 * k + 1], r]], axis=0)
                    units[m].product(totals[m][t % 2], w.at[:, k * 256 : (k + 1) * 256], v)

        def keep(t):
            for m in range(2):
                at = 0
                for total in totals[m][t % 2]:
                    n = total.shape[0]
                    qs[2 * t + m, at : at + n, :] = pltpu.matmul_pop(total)
                    at += n

        def out_row(y):
            for sp in range(2):
                total = None
                for a in range(3):
                    r = y - a + 1
                    if 0 <= r < rows:
                        at = (sp * 3 + a) * group
                        term = qs[r, at : at + group, :]
                        total = term if total is None else total + term
                back = (
                    shifted(total[:chans], -1)
                    + total[chans : 2 * chans]
                    + shifted(total[2 * chans :], 1)
                )
                emit(sp, y, back)

        for t in range(pairs + 2):
            if t < pairs:
                issue(t)
            if 1 <= t < pairs + 1:
                keep(t - 1)
            for y in (2 * t - 5, 2 * t - 4):
                if 0 <= y < rows:
                    out_row(y)
        out_row(rows - 1)

    def backward(totals):
        def pair(p, carry):
            s0 = 2 * p

            def emit(sp, y, back):
                own = rest[s0 + sp, y * chans : (y + 1) * chans, :]
                put(sp, y, own - (weight * c_in) * back)

            back_rows(totals, [s0 + j for j in range(span + 1)], wt1, emit)
            for sp in range(2):
                for j in range(cols // 128):
                    out[s0 + sp, :, j * 128 : (j + 1) * 128] = stage[sp, j]
            return carry

        lax.fori_loop(0, frames // 2, pair, 0)

        for side in range(2):
            first = half if side == 0 else frames
            lanes = (span - 1) * hid if side == 0 else 0
            back_rows(totals, [first, first + 1], wt1.at[:, lanes : lanes + 2 * hid], put)
            for sp in range(2):
                for j in range(cols // 128):
                    sent[2 * side + sp, :, j * 128 : (j + 1) * 128] = stage[sp, j].astype(BF16)

    pl.run_scoped(backward, [sums(m, 2 * group, 3) for m in range(2)])


def local(cw, b2s, noisy, before, after, observed, obs_mask, obs_channel, wf, b1, ws):
    frames, size, cols = noisy.shape
    rows = observed.shape[1]
    chans = size // rows
    hid = wf.shape[1]
    span = wf.shape[0] // (9 * chans)
    half = span // 2
    depth = -(-span * 9 * chans // 256) * 256
    dims = (frames, chans, rows, cols, hid, span)
    vmem = pl.BlockSpec(memory_space=pltpu.VMEM)
    smem = pl.BlockSpec(memory_space=pltpu.SMEM)
    return pl.pallas_call(
        functools.partial(main_kernel, dims),
        out_shape=(
            jax.ShapeDtypeStruct((frames, size, cols), F32),
            jax.ShapeDtypeStruct((2 * half, size, cols), BF16),
        ),
        in_specs=[smem, smem] + [vmem] * 9,
        out_specs=(vmem, vmem),
        scratch_shapes=[
            pltpu.VMEM((hid, depth), BF16),
            pltpu.VMEM((12 * chans, 2 * hid), BF16),
            pltpu.VMEM((2 * hid, 2 * hid), BF16),
            pltpu.VMEM((18 * chans, (span + 1) * hid), BF16),
            pltpu.VMEM((frames + 2 * half, (rows + 2) * 3 * chans, cols), BF16),
            pltpu.VMEM((frames, size, cols), BF16),
            pltpu.VMEM((2, rows, hid, cols), F32),
            pltpu.VMEM((2, rows // 2, 12 * chans, cols), F32),
            pltpu.VMEM((2, 2 * hid, cols), BF16),
            pltpu.VMEM(((rows + 2) * 3 * chans + 2 * hid, cols), BF16),
            pltpu.VMEM((frames + 2 * half, rows, hid, cols), BF16),
            pltpu.VMEM((rows, 18 * chans, cols), F32),
            pltpu.VMEM((frames, size, cols), F32),
            pltpu.VMEM((2, cols // 128, size, 128), F32),
        ],
        compiler_params=pltpu.CompilerParams(vmem_limit_bytes=56 << 20),
    )(cw, b2s, noisy, before, after, observed, obs_mask, obs_channel, wf, b1, ws)


def per_device(noisy, observed, obs_mask, obs_channel, step_index, w_first, b_first, w_second, b_second):
    frames, chans, rows, cols = noisy.shape
    hid = w_first.shape[0]
    span = w_first.shape[1] // chans
    half = span // 2
    size = chans * rows
    count = lax.axis_size("tm")
    up = [(i, i + 1) for i in range(count - 1)]
    down = [(i + 1, i) for i in range(count - 1)]

    level = step_index[0].astype(F32) / F32(STEPS - 1)
    sigma = F32(sigma_low) * jnp.exp(jnp.log(F32(sigma_ratio)) * level)
    c_in = 1.0 / jnp.sqrt(1.0 + sigma * sigma)
    weight = 1.0 / (1.0 + sigma * sigma)
    cw = jnp.stack([c_in, weight])

    flat = noisy.reshape(frames, size, cols)
    before = lax.ppermute(flat[frames - half :], "tm", up)
    after = lax.ppermute(flat[:half], "tm", down)

    out, sent = local(
        cw,
        b_second,
        flat,
        before,
        after,
        observed,
        obs_mask,
        obs_channel,
        jnp.transpose(w_first, (2, 3, 1, 0)).reshape(9 * span * chans, hid),
        b_first.reshape(1, hid),
        jnp.transpose(w_second, (2, 3, 0, 1)).reshape(9 * chans, hid),
    )
    from_right = lax.ppermute(sent[:half], "tm", down).astype(F32)
    from_left = lax.ppermute(sent[half:], "tm", up).astype(F32)
    out = out.at[frames - half :].add(-(weight * c_in) * from_right)
    out = out.at[:half].add(-(weight * c_in) * from_left)
    return out.reshape(frames, chans, rows, cols)


def solution(mesh):
    return jax.shard_map(
        per_device,
        mesh=mesh,
        in_specs=(
            P(("groups", "tm"), None, None, None),
            P(("groups", "tm"), None, None),
            P(("groups", "tm"), None, None),
            P(("groups", "tm"), None, None),
            P("groups"),
            P(),
            P(),
            P(),
            P(),
        ),
        out_specs=P(("groups", "tm"), None, None, None),
        check_vma=False,
    )
```

time: 103 us -> 60 us (0.58)
  Pallas kernels: 74 us -> 31 us
    pallas_call x1, Pallas kernels: 74 us -> 31 us  [local(): pl.pallas_call(functools.partial(main_kernel, dims), out_shape=(jax.Shape...]
  transfers between devices with their start and end apart: 4 -> 4, of which waited for: 3 -> 3; matrix products, arithmetic and copies ran while one was open for 2% -> 4% of each run, Pallas kernels for 0% -> 0%
where the time goes in v2:
time: 60 us; the launch traced here: 59.6 us
  Pallas kernels  31 us (52%)
  starting transfers between devices  12 us (20%)
  waiting for transfers between devices  8.57 us (14%)
  other arithmetic  4.38 us (7%)
  local copies, waits for them, and re-layouts  2.83 us (5%)
  between operations  0.82 us (1%)
    pallas_call x1, Pallas kernels, local(): pl.pallas_call(functools.partial(main_kernel, dims), out_shape=(jax.Shape...  31 us
    ppermute x1, starting transfers between devices, per_device(): before = lax.ppermute(flat[frames - half:], 'tm', up)  4.51 us
    ppermute x1, waiting for transfers between devices, per_device(): after = lax.ppermute(flat[:half], 'tm', down)  4.38 us
    ppermute x1, starting transfers between devices, per_device(): from_left = lax.ppermute(sent[half:], 'tm', up).astype(F32)  3.64 us
    ppermute x1, waiting for transfers between devices, per_device(): from_right = lax.ppermute(sent[:half], 'tm', down).astype(F32)  2.11 us
    ppermute x1, waiting for transfers between devices, per_device(): from_left = lax.ppermute(sent[half:], 'tm', up).astype(F32)  2.08 us
    ppermute x1, starting transfers between devices, per_device(): from_right = lax.ppermute(sent[:half], 'tm', down).astype(F32)  1.92 us
    ppermute x1, starting transfers between devices, per_device(): after = lax.ppermute(flat[:half], 'tm', down)  1.92 us
  transfers between devices with their start and end apart: 4, of which 3 were waited for; matrix products, arithmetic and copies ran while one was open for 4% of the time, Pallas kernels for 0%

profile of v2, /device:TPU:1, one launch (start us, length us, event | category | flops | bytes accessed | tf_op | source)
XLA Modules:
  0.0 59.6 jit_solution(6676297873884130940)
XLA Ops:
  0.0 1.1 %fusion.1 = (bf16[2,16,16,256]{3,2,1,0:T(8,128)(2,1)S(1)}, bf16[2,16,16,256]{3,2,1,0:T(8,128)(2,1)S(1)}) fusion(bf16[8,16,16,256]{3,2,1,0:T(8,128)(2,1)} %param.13), kind=kLoop, calls=%fused_computation.4 | loop fusion | bytes 1048576 | tf_op jit(solution)/shard_map/slice | solution.py:414
  1.1 4.5 %collective-permute-start = (bf16[2,256,256]{2,1,0:T(8,128)(2,1)S(1)}, bf16[2,256,256]{2,1,0:T(8,128)(2,1)S(1)}, u32[]{:S(2)}, u32[]{:S(2)}) collective-permute-start(bf16[2,256,256]{2,1,0:T(8,128)(2,1)S(1)} %bitcast.14), channel_id=1, source_target_pairs={{0,1},{1,2},{2,3},{3,4},{4,5},{5,6},{6,7},{7,8},{8,9},{9,10},{10,1... | collective-permute-start | bytes 786440 | tf_op jit(solution)/shard_map/ppermute | solution.py:413
  5.6 1.9 %collective-permute-start.1 = (bf16[2,256,256]{2,1,0:T(8,128)(2,1)S(1)}, bf16[2,256,256]{2,1,0:T(8,128)(2,1)S(1)}, u32[]{:S(2)}, u32[]{:S(2)}) collective-permute-start(bf16[2,256,256]{2,1,0:T(8,128)(2,1)S(1)} %bitcast.13), channel_id=1, source_target_pairs={{1,0},{2,1},{3,2},{4,3},{5,4},{6,5},{7,6},{8,7},{9,8},{10,9},{11,1... | collective-permute-start | bytes 786440 | tf_op jit(solution)/shard_map/ppermute | solution.py:414
  8.3 0.6 %pad_maximum_fusion.cw = f32[2]{0:T(128)} fusion(f32[1]{0:T(128)S(6)} %div.6, f32[1]{0:T(128)S(6)} %sqrt.4), kind=kLoop, calls=%fused_computation.3 | loop fusion | flops 2 | bytes 16 | tf_op jit(solution)/shard_map/stack | solution.py:410
  8.9 0.0 collective-permute-done.before
  8.9 0.0 copy-start
  8.9 4.4 %collective-permute-done.1.after = bf16[2,256,256]{2,1,0:T(8,128)(2,1)S(1)} collective-permute-done((bf16[2,256,256]{2,1,0:T(8,128)(2,1)S(1)}, bf16[2,256,256]{2,1,0:T(8,128)(2,1)S(1)}, u32[]{:S(2)}, u32[]{:S(2)}) %collective-permute-start.1) | collective-permute-done | bytes 262176 | tf_op jit(solution)/shard_map/ppermute | solution.py:414
  13.3 0.0 copy-start.1
  13.3 0.0 copy-done
  13.3 0.7 %copy-done.1 = bf16[2,256,256]{2,1,0:T(8,128)(2,1)} copy-done((bf16[2,256,256]{2,1,0:T(8,128)(2,1)}, bf16[2,256,256]{2,1,0:T(8,128)(2,1)S(1)}, u32[]{:S(2)}) %copy-start.1) | copy-done | bytes 262168
  14.0 31.0 %shard_map.91 = (f32[8,256,256]{2,1,0:T(8,128)}, bf16[4,256,256]{2,1,0:T(8,128)(2,1)}) custom-call(f32[2]{0:T(128)} %pad_maximum_fusion.cw, f32[16]{0:T(128)} %b2s.1, bf16[8,256,256]{2,1,0:T(8,128)(2,1)} %bitcast.12, bf16[2,256,256]{2,1,0:T(8,128)(2,1)} %copy-done, bf16[2,256,256]{2,1,0:T(8,128)(2,1)} %copy-done.1, f32[8,16,256]{2,1,0:T(8,128)} %obs.1, ...), custom_call_target="tpu_custom_call" | custom-call | tf_op jit(solution)/shard_map/pallas_call | solution.py:368
  45.0 1.1 %fusion.2 = (bf16[2,256,256]{2,1,0:T(8,128)(2,1)S(1)}, bf16[2,256,256]{2,1,0:T(8,128)(2,1)S(1)}) fusion(bf16[4,256,256]{2,1,0:T(8,128)(2,1)} %get-tuple-element.32), kind=kLoop, calls=%fused_computation.5 | loop fusion | bytes 1048576 | tf_op jit(solution)/shard_map/slice | solution.py:430
  46.1 1.9 %collective-permute-start.2 = (bf16[2,256,256]{2,1,0:T(8,128)(2,1)S(1)}, bf16[2,256,256]{2,1,0:T(8,128)(2,1)S(1)}, u32[]{:S(2)}, u32[]{:S(2)}) collective-permute-start(bf16[2,256,256]{2,1,0:T(8,128)(2,1)S(1)} %get-tuple-element.36), channel_id=1, source_target_pairs={{1,0},{2,1},{3,2},{4,3},{5,4},{6,5},{7,6},{8,7},{9,8},{10,9},{11,1... | collective-permute-start | bytes 786440 | tf_op jit(solution)/shard_map/ppermute | solution.py:429
  48.0 3.6 %collective-permute-start.3 = (bf16[2,256,256]{2,1,0:T(8,128)(2,1)S(1)}, bf16[2,256,256]{2,1,0:T(8,128)(2,1)S(1)}, u32[]{:S(2)}, u32[]{:S(2)}) collective-permute-start(bf16[2,256,256]{2,1,0:T(8,128)(2,1)S(1)} %get-tuple-element.35), channel_id=1, source_target_pairs={{0,1},{1,2},{2,3},{3,4},{4,5},{5,6},{6,7},{7,8},{8,9},{9,10},{10,1... | collective-permute-start | bytes 786440 | tf_op jit(solution)/shard_map/ppermute | solution.py:430
  51.7 2.1 %collective-permute-done.2 = bf16[2,256,256]{2,1,0:T(8,128)(2,1)S(1)} collective-permute-done((bf16[2,256,256]{2,1,0:T(8,128)(2,1)S(1)}, bf16[2,256,256]{2,1,0:T(8,128)(2,1)S(1)}, u32[]{:S(2)}, u32[]{:S(2)}) %collective-permute-start.2) | collective-permute-done | bytes 262176 | tf_op jit(solution)/shard_map/ppermute | solution.py:429
  53.8 1.9 %add_dynamic-update-slice_fusion = f32[8,256,256]{2,1,0:T(8,128)} fusion(f32[8,256,256]{2,1,0:T(8,128)} %get-tuple-element.31, bf16[2,256,256]{2,1,0:T(8,128)(2,1)S(1)} %collective-permute-done.2, f32[]{:T(128)} %bitcast.8), kind=kLoop, calls=%fused_computation.2 | loop fusion | flops 393216 | bytes 1311232 | tf_op jit(solution)/shard_map/scatter-add | solution.py:431
  55.7 2.1 %collective-permute-done.3 = bf16[2,256,256]{2,1,0:T(8,128)(2,1)S(1)} collective-permute-done((bf16[2,256,256]{2,1,0:T(8,128)(2,1)S(1)}, bf16[2,256,256]{2,1,0:T(8,128)(2,1)S(1)}, u32[]{:S(2)}, u32[]{:S(2)}) %collective-permute-start.3) | collective-permute-done | bytes 262176 | tf_op jit(solution)/shard_map/ppermute | solution.py:430
  57.7 1.9 %fusion = f32[8,256,256]{2,1,0:T(8,128)} fusion(f32[8,256,256]{2,1,0:T(8,128)} %add_dynamic-update-slice_fusion, bf16[2,256,256]{2,1,0:T(8,128)(2,1)S(1)} %collective-permute-done.3, f32[]{:T(128)} %bitcast.8), kind=kLoop, calls=%fused_computation.1 | loop fusion | flops 393216 | bytes 1311232 | tf_op jit(solution)/shard_map/scatter-add | solution.py:432
Async XLA Ops:
  1.1 7.8 %collective-permute-start = (bf16[2,256,256]{2,1,0:T(8,128)(2,1)S(1)}, bf16[2,256,256]{2,1,0:T(8,128)(2,1)S(1)}, u32[]{:S(2)}, u32[]{:S(2)}) collective-permute-start(bf16[2,256,256]{2,1,0:T(8,128)(2,1)S(1)} %bitcast.14), channel_id=1, source_target_pairs={{0,1},{1,2},{2,3},{3,4},{4,5},{5,6},{6,7},{7,8},{8,9},{9,10},{10,1... | collective-permute-start | bytes 786440 | tf_op jit(solution)/shard_map/ppermute | solution.py:413
  5.6 7.7 %collective-permute-start.1 = (bf16[2,256,256]{2,1,0:T(8,128)(2,1)S(1)}, bf16[2,256,256]{2,1,0:T(8,128)(2,1)S(1)}, u32[]{:S(2)}, u32[]{:S(2)}) collective-permute-start(bf16[2,256,256]{2,1,0:T(8,128)(2,1)S(1)} %bitcast.13), channel_id=1, source_target_pairs={{1,0},{2,1},{3,2},{4,3},{5,4},{6,5},{7,6},{8,7},{9,8},{10,9},{11,1... | collective-permute-start | bytes 786440 | tf_op jit(solution)/shard_map/ppermute | solution.py:414
  8.9 4.4 %copy-start = (bf16[2,256,256]{2,1,0:T(8,128)(2,1)}, bf16[2,256,256]{2,1,0:T(8,128)(2,1)S(1)}, u32[]{:S(2)}) copy-start(bf16[2,256,256]{2,1,0:T(8,128)(2,1)S(1)} %collective-permute-done.before) | copy-start | bytes 786436
  13.3 0.7 %copy-start.1 = (bf16[2,256,256]{2,1,0:T(8,128)(2,1)}, bf16[2,256,256]{2,1,0:T(8,128)(2,1)S(1)}, u32[]{:S(2)}) copy-start(bf16[2,256,256]{2,1,0:T(8,128)(2,1)S(1)} %collective-permute-done.1.after) | copy-start | bytes 786436
  46.1 7.7 %collective-permute-start.2 = (bf16[2,256,256]{2,1,0:T(8,128)(2,1)S(1)}, bf16[2,256,256]{2,1,0:T(8,128)(2,1)S(1)}, u32[]{:S(2)}, u32[]{:S(2)}) collective-permute-start(bf16[2,256,256]{2,1,0:T(8,128)(2,1)S(1)} %get-tuple-element.36), channel_id=1, source_target_pairs={{1,0},{2,1},{3,2},{4,3},{5,4},{6,5},{7,6},{8,7},{9,8},{10,9},{11,1... | collective-permute-start | bytes 786440 | tf_op jit(solution)/shard_map/ppermute | solution.py:429
  48.0 9.7 %collective-permute-start.3 = (bf16[2,256,256]{2,1,0:T(8,128)(2,1)S(1)}, bf16[2,256,256]{2,1,0:T(8,128)(2,1)S(1)}, u32[]{:S(2)}, u32[]{:S(2)}) collective-permute-start(bf16[2,256,256]{2,1,0:T(8,128)(2,1)S(1)} %get-tuple-element.35), channel_id=1, source_target_pairs={{0,1},{1,2},{2,3},{3,4},{4,5},{5,6},{6,7},{7,8},{8,9},{9,10},{10,1... | collective-permute-start | bytes 786440 | tf_op jit(solution)/shard_map/ppermute | solution.py:430

commit v3 on v0

v3 whole, which is shorter than its diff:
```python
import functools

import jax
import jax.numpy as jnp
import numpy as np
from jax import lax
from jax.experimental import pallas as pl
from jax.experimental.pallas import tpu as pltpu
from jax.sharding import PartitionSpec as P

STEPS = 64
sigma_low = 0.1
sigma_ratio = 20.0
F32 = jnp.float32
BF16 = jnp.bfloat16
CHUNK = 32


def shifted(x, by):
    lanes = x.shape[1]
    lane = lax.broadcasted_iota(jnp.int32, x.shape, 1)
    edge = 0 if by > 0 else lanes - 1
    return jnp.where(lane == edge, 0.0, pltpu.roll(x, by % lanes, 1))


def sums_for(unit, size, cols, n, copies=2):
    return [[pltpu.ACC(unit)((size, cols), F32) for _ in range(n)] for _ in range(copies)]


def level_rows(step, cols):
    level = jnp.full((1, cols), step, jnp.int32).astype(F32) / F32(STEPS - 1)
    sigma = F32(sigma_low) * jnp.exp(F32(np.log(sigma_ratio)) * level)
    square = 1.0 + sigma * sigma
    return 1.0 / jnp.sqrt(square), 1.0 / square


class Copy:

    def __init__(self, make):
        self.make = make

    def start(self):
        self.make().start()

    def wait(self):
        self.make().wait()


class Unit:

    def __init__(self, index):
        self.index = index
        self.turn = 0

    def steps(self, sums, left, right):
        slot = self.turn
        self.turn = 1 - slot
        work = [lambda: pltpu.matmul_push_rhs(right(), slot, self.index)]
        at = 0
        for n, total in enumerate(sums):
            size = total.shape[0]

            def add(total=total, at=at, size=size, first=n == 0):
                pltpu.matmul_acc_lhs(
                    total, left[at : at + size, :], load_staged_rhs=slot if first else None
                )

            work.append(add)
            at += size
        return work

    def product(self, sums, left, right):
        for piece in self.steps(sums, left, lambda: right):
            piece()


def weave(*lists):
    keyed = []
    for which, pieces in enumerate(lists):
        for n, piece in enumerate(pieces):
            keyed.append(((n + 0.5) / len(pieces), which, n, piece))
    for entry in sorted(keyed, key=lambda e: e[:3]):
        entry[3]()


def build_weights(dims, wf, b1, ws, w1, w2, w2t, wt1):
    frames, chans, rows, cols, hid, span = dims
    half = span // 2
    taps = 9 * chans
    group = 3 * chans

    def first_block(k, ab):
        at = (ab * span + k) * chans
        return wf[at : at + chans, :]

    blocks = [first_block(k, ab) for k in range(span) for ab in range(9)]
    bias = b1[...]
    high = bias.astype(BF16)
    left = bias - high.astype(F32)
    mid = left.astype(BF16)
    low = (left - mid.astype(F32)).astype(BF16)
    depth = w1.shape[1]
    tail = depth - span * taps
    sub = lax.broadcasted_iota(jnp.int32, (tail, hid), 0)
    extra = jnp.where(
        sub == 0,
        high.astype(F32),
        jnp.where(sub == 1, mid.astype(F32), jnp.where(sub == 2, low.astype(F32), 0.0)),
    )
    blocks.append(extra.astype(BF16))
    stacked = jnp.concatenate(blocks, axis=0).astype(F32) * 0.5
    w1[...] = stacked.T.astype(BF16)
    second = ws[...]
    zero_group = jnp.zeros((group, hid), BF16)

    def second_block(a):
        return second[a * group : (a + 1) * group, :] if 0 <= a < 3 else zero_group

    for o in range(4):
        for i in range(2):
            w2[o * group : (o + 1) * group, i * hid : (i + 1) * hid] = second_block(i + 2 - o)
    for i in range(2):
        tall = [second_block(i + 2 - m) for m in range(4)]
        tall.append(jnp.zeros((2 * hid - 4 * group, hid), BF16))
        tall = jnp.concatenate(tall, axis=0).astype(F32) * 0.5
        w2t[i * hid : (i + 1) * hid, :] = tall.T.astype(BF16)
    for sp in range(2):
        for ab in range(9):
            for tp in range(span + 1):
                k = sp - tp + 2 * half
                at = (sp * 9 + ab) * chans
                piece = first_block(k, ab) if 0 <= k < span else jnp.zeros((chans, hid), BF16)
                wt1[at : at + chans, tp * hid : (tp + 1) * hid] = piece


def reorder_frames(dims, units, c_in, perm, wide, jobs, loops):
    frames, chans, rows, cols, hid, span = dims
    group = 3 * chans
    size = chans * rows
    i0 = lax.broadcasted_iota(jnp.int32, (size, size), 0)
    i1 = lax.broadcasted_iota(jnp.int32, (size, size), 1)
    perm[...] = jnp.where((i0 % chans) * rows + i0 // chans == i1, 1.0, 0.0).astype(BF16)
    zero = jnp.zeros((group, cols), BF16)

    def spread(x, slot, y0):
        scaled = (c_in * x).astype(BF16).astype(F32)
        shifts = [shifted(scaled, 1).astype(BF16), scaled.astype(BF16), shifted(scaled, -1).astype(BF16)]
        for y in range(x.shape[0] // chans):
            for b in range(3):
                at = (y0 + y + 1) * group + b * chans
                wide[slot, at : at + chans, :] = shifts[b][y * chans : (y + 1) * chans, :]

    def run(totals):
        def step(j, carry):
            for m in range(2):
                source, slot, keep = jobs(j, m)
                units[m].product(totals[m], perm, source())
                wide[slot, 0:group, :] = zero
                wide[slot, (rows + 1) * group :, :] = zero
            for m in range(2):
                source, slot, keep = jobs(j, m)
                at = 0
                for total in totals[m]:
                    x = pltpu.matmul_pop(total)
                    keep(at, x)
                    spread(x, slot, at // chans)
                    at += x.shape[0]
            return carry

        lax.fori_loop(0, loops, step, 0)

    pl.run_scoped(run, [sums_for(m, size // 4, cols, 4, 1)[0] for m in range(2)])


def forward_frames(
    dims, units, weight, b2s, w1, w2, w2t, wide, nperm, obs, mask, chan, deriv, part, acts, mis, grads, rest, count, where,
    need, done, noisy0,
):
    frames, chans, rows, cols, hid, span = dims
    group = 3 * chans
    pairs = rows // 2
    depth = w1.shape[1]
    tail = depth - span * 9 * chans
    sub = lax.broadcasted_iota(jnp.int32, (tail, cols), 0)
    ones = jnp.where(sub < 3, 1.0, 0.0).astype(BF16)
    row_c = lax.broadcasted_iota(jnp.int32, (chans, cols), 0)
    b2 = jnp.zeros((chans, cols), F32)
    for c in range(chans):
        b2 = jnp.where(row_c == c, b2s[c], b2)
    mis[...] = jnp.zeros(mis.shape, BF16)

    def forward(sums1, sums2, sums3):

        def issue_first(f, t):
            work = []
            for k in range(depth // cols):
                for m in range(2):
                    r = 2 * t + m

                    def right(k=k, r=r):
                        pieces = [wide[where(f)[1] + b, r * group : (r + 3) * group, :] for b in range(span)]
                        v = jnp.concatenate(pieces + [ones], axis=0)
                        return v[k * 256 : (k + 1) * 256, :]

                    work.append(units[m].steps(sums1[m][t % 2], w1.at[:, k * 256 : (k + 1) * 256], right))
            return [piece for a, b in zip(work[0::2], work[1::2]) for both in zip(a, b) for piece in both]

        def activate(t, save):
            work = []
            for m in range(2):
                at = 0
                for total in sums1[m][t % 2]:

                    def piece(m=m, at=at, total=total):
                        h = pltpu.matmul_pop(total)
                        u = 1.0 + jnp.tanh(h)
                        act = h * u
                        deriv[save][2 * t + m, at : at + h.shape[0], :] = u * (1.0 + (h + h) - act)
                        acts[t % 2, m * hid + at : m * hid + at + h.shape[0], :] = act.astype(BF16)

                    work.append(piece)
                    at += total.shape[0]
            return work

        def issue_second(t):
            return units[0].steps(sums2[t % 2], w2, lambda: acts[t % 2])

        def keep_second(t, save):
            def piece(o):
                part[save][t, o * group : (o + 1) * group, :] = pltpu.matmul_pop(sums2[t % 2][o])

            return [functools.partial(piece, o) for o in range(4)]

        def misfit_row(g, y, load):
            t, i = y // 2, y % 2
            total = part[load][t, (1 + i) * group : (2 + i) * group, :]
            other, o = (t + 1, 0) if i else (t - 1, 3)
            if 0 <= other < pairs:
                total = total + part[load][other, o * group : (o + 1) * group, :]
            conv = shifted(total[:chans], 1) + total[chans : 2 * chans] + shifted(total[2 * chans :], -1)
            den = nperm[noisy0 + where(g)[0], y * chans : (y + 1) * chans, :].astype(F32) + conv + b2
            seen = mask[where(g)[0], y : y + 1, :]
            code = jnp.where(seen == 1, chan[where(g)[0], y : y + 1, :], -1)
            miss = jnp.where(row_c == code, den - obs[where(g)[0], y : y + 1, :], 0.0)
            rest[where(g)[3], y * chans : (y + 1) * chans, :] = den - weight * miss
            at = (y + 1) * group
            mis[g % 2, at : at + chans, :] = shifted(miss, -1).astype(BF16)
            mis[g % 2, at + chans : at + 2 * chans, :] = miss.astype(BF16)
            mis[g % 2, at + 2 * chans : at + 3 * chans, :] = shifted(miss, 1).astype(BF16)

        def issue_third(g, q):
            at = 2 * q * group
            return units[1].steps(sums3[q % 2], w2t, lambda: mis[g % 2, at : at + 2 * hid, :])

        def keep_third(g, q, load):
            work = []
            at = 0
            for total in sums3[q % 2]:

                def piece(at=at, total=total):
                    n = total.shape[0]
                    i, low = at // hid, at % hid
                    y = 2 * q + i
                    d = pltpu.matmul_pop(total) * deriv[load][y, low : low + n, :]
                    grads[where(g)[2], y, low : low + n, :] = d.astype(BF16)

                work.append(piece)
                at += total.shape[0]
            return work

        total = count * pairs
        lag = 6
        for n in range(total + lag + 2):
            first, small, vector = [], [], []
            if 2 <= n < total + 2:
                small += issue_second((n - 2) % pairs)
            q = n - lag - 1
            if 0 <= q < total:
                small += issue_third(q // pairs, q % pairs)
            if n < total:
                if n % pairs == 0:
                    need(n // pairs)
                first += issue_first(n // pairs, n % pairs)
            if 1 <= n < total + 1:
                vector.append(activate((n - 1) % pairs, (n - 1) // pairs % 2))
            if 3 <= n < total + 3:
                vector.append(keep_second((n - 3) % pairs, (n - 3) // pairs % 2))
            q = n - lag + 1
            if 0 <= q < total:
                g, t = q // pairs, q % pairs
                ys = ([2 * t - 1] if t else []) + [2 * t] + ([rows - 1] if t == pairs - 1 else [])
                vector.append([functools.partial(misfit_row, g, y, g % 2) for y in ys])
            q = n - lag - 2
            if q >= 0:
                vector.append(keep_third(q // pairs, q % pairs, q // pairs % 2))
            weave(small + first, *vector)
            if q >= 0 and q % pairs == pairs - 1:
                done(q // pairs)

    pl.run_scoped(
        forward,
        [sums_for(m, CHUNK, cols, hid // CHUNK) for m in range(2)],
        sums_for(0, group, cols, 4),
        sums_for(1, CHUNK, cols, 2 * hid // CHUNK),
    )


def backward_frames(dims, units, scale, wt1, grads, qs, rest, stage, out, first, done):
    frames, chans, rows, cols, hid, span = dims
    group = 3 * chans
    pairs = rows // 2

    def put(p, sp, y, value):
        for j in range(cols // 128):
            stage[p % 2, sp, j, pl.ds(y, chans, stride=rows), :] = value[:, j * 128 : (j + 1) * 128]

    def issue(totals, p, t):
        work = []
        for k in range((span + 1) // 2):
            for m in range(2):

                def right(r=2 * t + m, slot=2 * p + 2 * k):
                    return jnp.concatenate([grads[slot, r], grads[slot + 1, r]], axis=0)

                work.append(units[m].steps(totals[m][t % 2], wt1.at[:, k * 256 : (k + 1) * 256], right))
        return [piece for a, b in zip(work[0::2], work[1::2]) for both in zip(a, b) for piece in both]

    def keep(totals, p, t):
        work = []
        for m in range(2):
            at = 0
            for total in totals[m][t % 2]:

                def piece(m=m, at=at, total=total):
                    qs[p % 2, 2 * t + m, at : at + total.shape[0], :] = pltpu.matmul_pop(total)

                work.append(piece)
                at += total.shape[0]
        return work

    def out_row(p, y, sp):
        total = None
        for a in range(3):
            r = y - a + 1
            if 0 <= r < rows:
                at = (sp * 3 + a) * group
                term = qs[p % 2, r, at : at + group, :]
                total = term if total is None else total + term
        back = shifted(total[:chans], -1) + total[chans : 2 * chans] + shifted(total[2 * chans :], 1)
        own = rest[first + 2 * p + sp, y * chans : (y + 1) * chans, :]
        put(p, sp, y, own - scale * back)

    def store(p):
        for sp in range(2):
            for j in range(cols // 128):
                out[2 * p + sp, :, j * 128 : (j + 1) * 128] = stage[p % 2, sp, j]

    def backward(totals):
        steps = frames // 2 * pairs
        for n in range(steps + 2):
            lists = []
            if n < steps:
                lists.append(issue(totals, n // pairs, n % pairs))
            q = n - 1
            if 0 <= q < steps:
                lists.append(keep(totals, q // pairs, q % pairs))
            q = n - 2
            if q >= 0:
                p, t = q // pairs, q % pairs
                ys = ([2 * t - 1] if t else []) + [2 * t] + ([rows - 1] if t == pairs - 1 else [])
                lists.append([functools.partial(out_row, p, y, sp) for y in ys for sp in range(2)])
            weave(*lists)
            if q >= 0 and t == pairs - 1:
                store(p)
                done(p)

    pl.run_scoped(backward, [sums_for(m, group, cols, 6) for m in range(2)])


def pack_kernel(dims, noisy, obs, mask, chan, up, down, planes, obs_s, mask_s, chan_s, sems):
    frames, chans, rows, cols, hid, span = dims
    half = span // 2
    size = chans * rows
    own = 2 * half
    ends = ((up, frames - own, frames - half), (down, 0, 0))
    copies = []

    def copy(src, dst, n):
        copies.append(pltpu.make_async_copy(src, dst, sems.at[n]))
        copies[-1].start()

    for d, (to, first, frame0) in enumerate(ends):
        for n, (src, dst) in enumerate(((obs, obs_s), (mask, mask_s), (chan, chan_s))):
            copy(src.at[pl.ds(frame0, half)], dst.at[d], 4 * d + n)
    for d, (to, first, frame0) in enumerate(ends):
        for n in range(own):
            copy(noisy.at[first + n], planes.at[d, pl.ds(n * size, size)], 8 + own * d + n)
    for c in copies[:6]:
        c.wait()
    for d in range(2):
        at = own * size
        for n in range(half):
            seen = mask_s[d, n].astype(F32).astype(BF16)
            which = chan_s[d, n].astype(F32).astype(BF16)
            value = obs_s[d, n]
            high = value.astype(BF16)
            left = value - high.astype(F32)
            mid = left.astype(BF16)
            low = (left - mid.astype(F32)).astype(BF16)
            for plane in (seen, which, high, mid, low):
                planes[d, at : at + rows, :] = plane
                at += rows
    for d in range(2):
        for c in copies[6 + own * d : 6 + own * (d + 1)]:
            c.wait()
        copy(planes.at[d], ends[d][0], 4 * d + 3)
    for c in copies[-2:]:
        c.wait()


def inner_kernel(
    dims, step, b2s, noisy, obs, mask, chan, wf, b1, ws,
    wide_out, nperm_out, grads_out, rest_out, w1_out, w2_out, w2t_out, wt1_out,
    w1, w2, w2t, wt1, perm, wide, nperm, noisy_s, obs_s, mask_s, chan_s, deriv0, deriv1, part0, part1, acts, mis,
    grads, rest, sems,
):
    frames, chans, rows, cols, hid, span = dims
    half = span // 2
    inner = frames - 2 * half
    units = (Unit(0), Unit(1))
    c_in, weight = level_rows(step[0], cols)
    arriving = [
        Copy(
            lambda n=n: pltpu.make_async_copy(
                noisy.at[pl.ds(2 * n, 2)], noisy_s.at[pl.ds(2 * n, 2)], sems.at[n]
            )
        )
        for n in range(frames // 2)
    ]
    for a, b in ((obs, obs_s), (mask, mask_s), (chan, chan_s)):
        at = len(arriving)
        arriving.append(
            Copy(lambda a=a, b=b, at=at: pltpu.make_async_copy(a.at[pl.ds(half, inner)], b, sems.at[at]))
        )
    for c in arriving:
        c.start()
    copies = []

    def leave(a, b, i=None):
        at = len(arriving) + len(copies)

        def make():
            if i is None:
                return pltpu.make_async_copy(a, b, sems.at[at])
            return pltpu.make_async_copy(a.at[i], b.at[i], sems.at[at])

        copies.append(Copy(make))
        copies[-1].start()

    build_weights(dims, wf, b1, ws, w1, w2, w2t, wt1)
    for a, b in ((w1, w1_out), (w2, w2_out), (w2t, w2t_out), (wt1, wt1_out)):
        leave(a, b)

    def jobs(j, m):
        f = 2 * j + m

        def keep(at, x):
            nperm[f, at : at + x.shape[0], :] = x.astype(BF16)

        return (lambda: noisy_s[f]), f, keep

    for c in arriving[: frames // 2]:
        c.wait()
    reorder_frames(dims, units, c_in, perm, wide, jobs, frames // 2)
    leave(wide, wide_out)
    leave(nperm, nperm_out)
    for c in arriving[frames // 2 :]:
        c.wait()

    def done(i):
        leave(grads, grads_out, i)
        leave(rest, rest_out, i)

    forward_frames(
        dims, units, weight, b2s, w1, w2, w2t, wide, nperm, obs_s, mask_s, chan_s, (deriv0, deriv1), (part0, part1),
        acts, mis, grads, rest, inner, lambda i: (i, i, i, i), lambda i: None, done, half,
    )
    for copy in copies:
        copy.wait()


def outer_kernel(
    dims, step, b2s, obs, mask, chan, before, after,
    wide_in, nperm_in, grads_in, rest_in, w1_in, w2_in, w2t_in, wt1_in,
    out,
    w1, w2, w2t, wt1, perm, wide, nperm, before_s, after_s, seen, which, value, deriv0, deriv1, part0, part1, acts, mis,
    grads, rest, qs, stage, result, sems,
):
    frames, chans, rows, cols, hid, span = dims
    half = span // 2
    size = chans * rows
    own = 2 * half
    units = (Unit(0), Unit(1))
    inner = frames - 2 * half
    c_in, weight = level_rows(step[0], cols)
    copies = []

    def arrive(a, b, from_at=None, to_at=None, count=None):
        n = len(copies)

        def make():
            src = a if from_at is None else a.at[pl.ds(from_at, count)]
            dst = b if to_at is None else b.at[pl.ds(to_at, count)]
            return pltpu.make_async_copy(src, dst, sems.at[n])

        copies.append(Copy(make))
        copies[-1].start()

    arrive(before, before_s)
    arrive(after, after_s)
    for a, b in ((mask, seen), (chan, which), (obs, value)):
        arrive(a, b, 0, half, half)
        arrive(a, b, frames - half, 2 * half, half)
    for a, b in ((w1_in, w1), (w2_in, w2), (w2t_in, w2t)):
        arrive(a, b)
    arrive(nperm_in, nperm, 0, half, half)
    arrive(nperm_in, nperm, frames - half, 2 * half, half)
    early = len(copies)
    for n in range(frames):
        arrive(wide_in, wide, n, own + n, 1)
    wides = len(copies)
    arrive(wt1_in, wt1)
    arrive(grads_in, grads, 0, 2 * half, inner)
    arrive(rest_in, rest, 0, 2 * half, inner)

    def jobs(j, m):
        src = after_s if m else before_s
        slot = own + frames + j if m else j
        keeps = j < half if m else j >= half
        place = 3 * half + j if m else j - half

        def keep(at, x):
            @pl.when(keeps)
            def _():
                nperm[place, at : at + x.shape[0], :] = x.astype(BF16)

        return (lambda: src[pl.ds(pl.multiple_of(j * size, size), size), :]), slot, keep

    copies[0].wait()
    copies[1].wait()
    for n in range(half):
        for src, base in ((before_s, 0), (after_s, 3 * half)):
            at = own * size + 5 * rows * n
            planes = [src[at + rows * i : at + rows * (i + 1), :].astype(F32) for i in range(5)]
            seen[base + n] = planes[0].astype(jnp.int32)
            which[base + n] = planes[1].astype(jnp.int32)
            value[base + n] = planes[2] + (planes[3] + planes[4])
    reorder_frames(dims, units, c_in, perm, wide, jobs, own)
    for copy in copies[2:early]:
        copy.wait()

    def where(i):
        gap = inner if i >= 2 * half else 0
        return i, i + gap, i + gap, i + gap

    arrived = [0]

    def need(i):
        last = min(max(where(i)[1] + span - own, 0), frames)
        while arrived[0] < last:
            copies[early + arrived[0]].wait()
            arrived[0] += 1

    forward_frames(
        dims, units, weight, b2s, w1, w2, w2t, wide, nperm, value, seen, which, (deriv0, deriv1), (part0, part1),
        acts, mis, grads, rest, 4 * half, where, need, lambda i: None, 0,
    )
    for copy in copies[wides:]:
        copy.wait()
    leaving = []

    def done(p):
        at = len(copies) + len(leaving)
        leaving.append(
            Copy(
                lambda: pltpu.make_async_copy(
                    result.at[pl.ds(2 * p, 2)], out.at[pl.ds(2 * p, 2)], sems.at[at]
                )
            )
        )
        leaving[-1].start()

    backward_frames(dims, units, c_in * weight, wt1, grads, qs, rest, stage, result, half, done)
    for copy in leaving:
        copy.wait()


def per_device(noisy, observed, obs_mask, obs_channel, step_index, w_first, b_first, w_second, b_second):
    frames, chans, rows, cols = noisy.shape
    hid = w_first.shape[0]
    span = w_first.shape[1] // chans
    half = span // 2
    size = chans * rows
    inner = frames - 2 * half
    count = lax.axis_size("tm")
    up = [(i, i + 1) for i in range(count - 1)]
    down = [(i + 1, i) for i in range(count - 1)]

    depth = -(-span * 9 * chans // 256) * 256
    dims = (frames, chans, rows, cols, hid, span)
    vmem = pl.BlockSpec(memory_space=pltpu.VMEM)
    smem = pl.BlockSpec(memory_space=pltpu.SMEM)
    hbm = pl.BlockSpec(memory_space=pl.ANY)
    shape = jax.ShapeDtypeStruct

    flat = noisy.reshape(frames, size, cols)
    planes = 2 * half * size + 5 * half * rows
    to_up, to_down = pl.pallas_call(
        functools.partial(pack_kernel, dims),
        out_shape=(shape((planes, cols), BF16), shape((planes, cols), BF16)),
        in_specs=[hbm] * 4,
        out_specs=(hbm, hbm),
        scratch_shapes=[
            pltpu.VMEM((2, planes, cols), BF16),
            pltpu.VMEM((2, half, rows, cols), F32),
            pltpu.VMEM((2, half, rows, cols), jnp.int32),
            pltpu.VMEM((2, half, rows, cols), jnp.int32),
            pltpu.SemaphoreType.DMA((8 + 4 * half,)),
        ],
        compiler_params=pltpu.CompilerParams(vmem_limit_bytes=62 << 20),
    )(flat, observed, obs_mask, obs_channel)
    before = pltpu.with_memory_space_constraint(lax.ppermute(to_up, "tm", up), pltpu.HBM)
    after = pltpu.with_memory_space_constraint(lax.ppermute(to_down, "tm", down), pltpu.HBM)

    wf = jnp.transpose(w_first, (2, 3, 1, 0)).reshape(9 * span * chans, hid)
    ws = jnp.transpose(w_second, (2, 3, 0, 1)).reshape(9 * chans, hid)
    weights = [
        ((hid, depth), BF16),
        ((12 * chans, 2 * hid), BF16),
        ((2 * hid, 2 * hid), BF16),
        ((18 * chans, (span + 1) * hid), BF16),
    ]
    wide_rows = (rows + 2) * 3 * chans
    work = [
        pltpu.VMEM((rows, hid, cols), F32),
        pltpu.VMEM((rows, hid, cols), F32),
        pltpu.VMEM((rows // 2, 12 * chans, cols), F32),
        pltpu.VMEM((rows // 2, 12 * chans, cols), F32),
        pltpu.VMEM((2, 2 * hid, cols), BF16),
        pltpu.VMEM((2, wide_rows + 2 * hid, cols), BF16),
    ]
    kept = [
        ((frames, wide_rows, cols), BF16),
        ((frames, size, cols), BF16),
        ((inner, rows, hid, cols), BF16),
        ((inner, size, cols), F32),
    ]
    flops = 2 * 9 * rows * cols * hid * chans * (span + 2) * inner
    results = pl.pallas_call(
        functools.partial(inner_kernel, dims),
        out_shape=tuple(shape(*k) for k in kept + weights),
        in_specs=[smem, smem] + [hbm] * 4 + [vmem] * 3,
        out_specs=(hbm,) * 8,
        scratch_shapes=[pltpu.VMEM(*w) for w in weights]
        + [pltpu.VMEM((size, size), BF16), pltpu.VMEM(*kept[0]), pltpu.VMEM(*kept[1])]
        + [pltpu.VMEM((frames, size, cols), BF16)]
        + [pltpu.VMEM((inner, rows, cols), t) for t in (F32, jnp.int32, jnp.int32)]
        + work
        + [pltpu.VMEM(*kept[2]), pltpu.VMEM(*kept[3]), pltpu.SemaphoreType.DMA((frames // 2 + 9 + 2 * inner,))],
        compiler_params=pltpu.CompilerParams(vmem_limit_bytes=62 << 20),
        cost_estimate=pl.CostEstimate(flops=4 * flops, bytes_accessed=12 << 20, transcendentals=0),
    )(step_index, b_second, flat, observed, obs_mask, obs_channel, wf, b_first.reshape(1, hid), ws)

    out = pl.pallas_call(
        functools.partial(outer_kernel, dims),
        out_shape=shape((frames, size, cols), F32),
        in_specs=[smem, smem] + [hbm] * 13,
        out_specs=hbm,
        scratch_shapes=[pltpu.VMEM(*w) for w in weights]
        + [
            pltpu.VMEM((size, size), BF16),
            pltpu.VMEM((frames + 4 * half, wide_rows, cols), BF16),
            pltpu.VMEM((4 * half, size, cols), BF16),
            pltpu.VMEM((planes, cols), BF16),
            pltpu.VMEM((planes, cols), BF16),
            pltpu.VMEM((4 * half, rows, cols), jnp.int32),
            pltpu.VMEM((4 * half, rows, cols), jnp.int32),
            pltpu.VMEM((4 * half, rows, cols), F32),
        ]
        + work
        + [
            pltpu.VMEM((frames + 2 * half, rows, hid, cols), BF16),
            pltpu.VMEM((frames + 2 * half, size, cols), F32),
            pltpu.VMEM((2, rows, 18 * chans, cols), F32),
            pltpu.VMEM((2, 2, cols // 128, size, 128), F32),
            pltpu.VMEM((frames, size, cols), F32),
            pltpu.SemaphoreType.DMA((16 + frames + frames // 2,)),
        ],
        compiler_params=pltpu.CompilerParams(vmem_limit_bytes=62 << 20),
    )(step_index, b_second, observed, obs_mask, obs_channel, before, after, *results)
    return out.reshape(frames, chans, rows, cols)


def solution(mesh):
    return jax.shard_map(
        per_device,
        mesh=mesh,
        in_specs=(
            P(("groups", "tm"), None, None, None),
            P(("groups", "tm"), None, None),
            P(("groups", "tm"), None, None),
            P(("groups", "tm"), None, None),
            P("groups"),
            P(),
            P(),
            P(),
            P(),
        ),
        out_specs=P(("groups", "tm"), None, None, None),
        check_vma=False,
    )
```

time: 172 us -> 52.6 us (0.31); the launches traced: 169 us -> 52.4 us
  matrix products: 84.9 us -> 0 us
  local copies, waits for them, and re-layouts: 46.8 us -> 1.02 us
  Pallas kernels: 0 us -> 44 us
  other arithmetic: 16.2 us -> 0 us
  waiting for transfers between devices: 8.02 us -> 0.01 us
  starting transfers between devices: 12.1 us -> 6.43 us
    conv_general_dilated x4 -> x0, matrix products: 84.9 us -> none  [conv(): lax.conv_general_dilated(value, kernel, (1, 1), ((1, 1), (1, 1)), dimensi...]
    pallas_call x0 -> x3, Pallas kernels: none -> 44 us  [the longest x1 29 us: per_device(): pl.pallas_call(functools.partial(outer_kernel, dims), out_shape=shape((fr...]
    conv_general_dilated x2 -> x0, local copies, waits for them, and re-layouts: 20 us -> none  [conv(): lax.conv_general_dilated(value, kernel, (1, 1), ((1, 1), (1, 1)), dimensi...]
    concatenate x1 -> x0, local copies, waits for them, and re-layouts: 8.99 us -> none  [stack_windows(): return jnp.concatenate([source[k:k + frames] for k in range(span)], axis=1)]
    ppermute x4 -> x2, waiting for transfers between devices: 8.02 us -> 0.01 us  [the longest x1 0.01 us: per_device(): lax.ppermute(to_up, 'tm', up)]
    convert_element_type x1 -> x0, local copies, waits for them, and re-layouts: 7.46 us -> none  [per_device(): misfit_b = misfit.astype(jnp.bfloat16)]
    unnamed x20 -> x4, local copies, waits for them, and re-layouts: 7.68 us -> 1.02 us
    ppermute x4 -> x2, starting transfers between devices: 12.1 us -> 6.43 us  [the longest x1 4.51 us: per_device(): lax.ppermute(to_up, 'tm', up)]
  transfers between devices with their start and end apart: 4 -> 2, of which waited for: 4 -> 0; matrix products, arithmetic and copies ran while one was open for 2% -> 0% of each run, Pallas kernels for 0% -> 24%
where the time goes in v3:
time: 52.6 us; the launch traced here: 52.4 us
  Pallas kernels  44 us (84%)
  starting transfers between devices  6.43 us (12%)
  local copies, waits for them, and re-layouts  1.02 us (2%)
  between operations  0.89 us (2%)
    pallas_call x1, Pallas kernels, per_device(): pl.pallas_call(functools.partial(outer_kernel, dims), out_shape=shape((fr...  29 us
    pallas_call x1, Pallas kernels, per_device(): pl.pallas_call(functools.partial(inner_kernel, dims), out_shape=tuple((sh...  12.6 us
    ppermute x1, starting transfers between devices, per_device(): lax.ppermute(to_up, 'tm', up)  4.51 us
    pallas_call x1, Pallas kernels, per_device(): pl.pallas_call(functools.partial(pack_kernel, dims), out_shape=(shape((pl...  2.4 us
    ppermute x1, starting transfers between devices, per_device(): lax.ppermute(to_down, 'tm', down)  1.92 us
  transfers between devices with their start and end apart: 2, of which 0 were waited for; matrix products, arithmetic and copies ran while one was open for 0% of the time, Pallas kernels for 24%

profile of v3, /device:TPU:1, one launch (start us, length us, event | category | flops | bytes accessed | tf_op | source)
XLA Modules:
  0.0 52.4 jit_solution(5336462001765523723)
XLA Ops:
  0.0 2.4 %shard_map.91 = (bf16[1184,256]{1,0:T(8,128)(2,1)}, bf16[1184,256]{1,0:T(8,128)(2,1)}) custom-call(bf16[8,256,256]{2,1,0:T(8,128)(2,1)} %bitcast.9, f32[8,16,256]{2,1,0:T(8,128)} %obs.5, s32[8,16,256]{2,1,0:T(8,128)} %mask.5, s32[8,16,256]{2,1,0:T(8,128)} %chan.5), custom_call_target="tpu_custom_call" | custom-call | tf_op jit(solution)/shard_map/pallas_call | solution.py:618
  2.4 4.5 %collective-permute-start = (bf16[1184,256]{1,0:T(8,128)(2,1)}, bf16[1184,256]{1,0:T(8,128)(2,1)S(1)}, u32[]{:S(2)}, u32[]{:S(2)}) collective-permute-start(bf16[1184,256]{1,0:T(8,128)(2,1)} %get-tuple-element.15), channel_id=1, source_target_pairs={{0,1},{1,2},{2,3},{3,4},{4,5},{5,6},{6,7},{7,8},{8,9},{9,10},{10,1... | collective-permute-start | bytes 1818632 | tf_op jit(solution)/shard_map/ppermute | solution.py:632
  6.9 1.9 %collective-permute-start.1 = (bf16[1184,256]{1,0:T(8,128)(2,1)}, bf16[1184,256]{1,0:T(8,128)(2,1)S(1)}, u32[]{:S(2)}, u32[]{:S(2)}) collective-permute-start(bf16[1184,256]{1,0:T(8,128)(2,1)} %get-tuple-element.16), channel_id=1, source_target_pairs={{1,0},{2,1},{3,2},{4,3},{5,4},{6,5},{7,6},{8,7},{9,8},{10,9},{11,1... | collective-permute-start | bytes 1818632 | tf_op jit(solution)/shard_map/ppermute | solution.py:633
  9.5 12.6 %shard_map.92 = (bf16[8,864,256]{2,1,0:T(8,128)(2,1)}, bf16[8,256,256]{2,1,0:T(8,128)(2,1)}, bf16[4,16,128,256]{3,2,1,0:T(8,128)(2,1)}, f32[4,256,256]{2,1,0:T(8...) custom-call(s32[1]{0:T(128)S(6)} %copy.10.step, ...), custom_call_target="tpu_custom_call" | custom-call | flops 16911433728 | bytes 12582912 | tf_op jit(solution)/shard_map/pallas_call | solution.py:659
  22.1 0.0 collective-permute-done.before
  22.1 0.0 copy-start
  22.1 0.0 collective-permute-done.1.after
  22.1 0.0 copy-start.1
  22.1 0.8 %copy-done = bf16[1184,256]{1,0:T(8,128)(2,1)} copy-done((bf16[1184,256]{1,0:T(8,128)(2,1)}, bf16[1184,256]{1,0:T(8,128)(2,1)S(1)}, u32[]{:S(2)}) %copy-start) | copy-done | bytes 606232
  22.9 0.2 copy-done.1
  23.1 29.0 %shard_map.93 = f32[8,256,256]{2,1,0:T(8,128)} custom-call(s32[1]{0:T(128)S(6)} %copy.10.step, f32[16]{0:T(128)} %b2s.3, f32[8,16,256]{2,1,0:T(8,128)} %obs.5, s32[8,16,256]{2,1,0:T(8,128)} %mask.5, s32[8,16,256]{2,1,0:T(8,128)} %chan.5, bf16[1184,256]{1,0:T(8,128)(2,1)} %copy-done, bf16[1184,256]{1,0:T(8,128)(2,1)} %copy-done.1, ...), custom_call_target="tpu_custom_call" | custom-call | tf_op jit(solution)/shard_map/pallas_call | solution.py:674
Async XLA Ops:
  2.4 19.7 %collective-permute-start = (bf16[1184,256]{1,0:T(8,128)(2,1)}, bf16[1184,256]{1,0:T(8,128)(2,1)S(1)}, u32[]{:S(2)}, u32[]{:S(2)}) collective-permute-start(bf16[1184,256]{1,0:T(8,128)(2,1)} %get-tuple-element.15), channel_id=1, source_target_pairs={{0,1},{1,2},{2,3},{3,4},{4,5},{5,6},{6,7},{7,8},{8,9},{9,10},{10,1... | collective-permute-start | bytes 1818632 | tf_op jit(solution)/shard_map/ppermute | solution.py:632
  6.9 15.2 %collective-permute-start.1 = (bf16[1184,256]{1,0:T(8,128)(2,1)}, bf16[1184,256]{1,0:T(8,128)(2,1)S(1)}, u32[]{:S(2)}, u32[]{:S(2)}) collective-permute-start(bf16[1184,256]{1,0:T(8,128)(2,1)} %get-tuple-element.16), channel_id=1, source_target_pairs={{1,0},{2,1},{3,2},{4,3},{5,4},{6,5},{7,6},{8,7},{9,8},{10,9},{11,1... | collective-permute-start | bytes 1818632 | tf_op jit(solution)/shard_map/ppermute | solution.py:633
  22.1 0.8 %copy-start = (bf16[1184,256]{1,0:T(8,128)(2,1)}, bf16[1184,256]{1,0:T(8,128)(2,1)S(1)}, u32[]{:S(2)}) copy-start(bf16[1184,256]{1,0:T(8,128)(2,1)S(1)} %collective-permute-done.before) | copy-start | bytes 1818628
  22.1 1.0 %copy-start.1 = (bf16[1184,256]{1,0:T(8,128)(2,1)}, bf16[1184,256]{1,0:T(8,128)(2,1)S(1)}, u32[]{:S(2)}) copy-start(bf16[1184,256]{1,0:T(8,128)(2,1)S(1)} %collective-permute-done.1.after) | copy-start | bytes 1818628

commit v4 on v3

--- a/solution.py
+++ b/solution.py
@@ -17,10 +17,12 @@
 
 
 def shifted(x, by):
-    lanes = x.shape[1]
-    lane = lax.broadcasted_iota(jnp.int32, x.shape, 1)
-    edge = 0 if by > 0 else lanes - 1
-    return jnp.where(lane == edge, 0.0, pltpu.roll(x, by % lanes, 1))
+    tiles = [x[:, at : at + 128] for at in range(0, x.shape[1], 128)]
+    lane = lax.broadcasted_iota(jnp.int32, tiles[0].shape, 1)
+    edge = lane == (0 if by > 0 else 127)
+    turned = [pltpu.roll(tile, by % 128, 1) for tile in tiles]
+    beyond = [0.0] + turned[:-1] if by > 0 else turned[1:] + [0.0]
+    return jnp.concatenate([jnp.where(edge, b, t) for b, t in zip(beyond, turned)], axis=1)
 
 
 def sums_for(unit, size, cols, n, copies=2):
@@ -151,25 +153,24 @@
                 wide[slot, at : at + chans, :] = shifts[b][y * chans : (y + 1) * chans, :]
 
     def run(totals):
-        def step(j, carry):
-            for m in range(2):
-                source, slot, keep = jobs(j, m)
-                units[m].product(totals[m], perm, source())
-                wide[slot, 0:group, :] = zero
-                wide[slot, (rows + 1) * group :, :] = zero
-            for m in range(2):
-                source, slot, keep = jobs(j, m)
-                at = 0
-                for total in totals[m]:
-                    x = pltpu.matmul_pop(total)
-                    keep(at, x)
-                    spread(x, slot, at // chans)
-                    at += x.shape[0]
-            return carry
-
-        lax.fori_loop(0, loops, step, 0)
-
-    pl.run_scoped(run, [sums_for(m, size // 4, cols, 4, 1)[0] for m in range(2)])
+        for n in range(loops + 1):
+            if n < loops:
+                for m in range(2):
+                    source, slot, keep = jobs(n, m)
+                    units[m].product(totals[m][n % 2], perm, source())
+                    wide[slot, 0:group, :] = zero
+                    wide[slot, (rows + 1) * group :, :] = zero
+            if n > 0:
+                for m in range(2):
+                    source, slot, keep = jobs(n - 1, m)
+                    at = 0
+                    for total in totals[m][(n - 1) % 2]:
+                        x = pltpu.matmul_pop(total)
+                        keep(at, x)
+                        spread(x, slot, at // chans)
+                        at += x.shape[0]
+
+    pl.run_scoped(run, [sums_for(m, size // 4, cols, 4) for m in range(2)])
 
 
 def forward_frames(
@@ -213,9 +214,10 @@
 
                     def piece(m=m, at=at, total=total):
                         h = pltpu.matmul_pop(total)
-                        u = 1.0 + jnp.tanh(h)
+                        th = jnp.tanh(h)
+                        u = 1.0 + th
                         act = h * u
-                        deriv[save][2 * t + m, at : at + h.shape[0], :] = u * (1.0 + (h + h) - act)
+                        deriv[save][2 * t + m, at : at + h.shape[0], :] = u + act * (1.0 - th)
                         acts[t % 2, m * hid + at : m * hid + at + h.shape[0], :] = act.astype(BF16)
 
                     work.append(piece)
@@ -377,7 +379,7 @@
     pl.run_scoped(backward, [sums_for(m, group, cols, 6) for m in range(2)])
 
 
-def pack_kernel(dims, noisy, obs, mask, chan, up, down, planes, obs_s, mask_s, chan_s, sems):
+def pack_kernel(dims, noisy, obs, mask, chan, up, down, obs_s, mask_s, chan_s, sems):
     frames, chans, rows, cols, hid, span = dims
     half = span // 2
     size = chans * rows
@@ -394,7 +396,7 @@
             copy(src.at[pl.ds(frame0, half)], dst.at[d], 4 * d + n)
     for d, (to, first, frame0) in enumerate(ends):
         for n in range(own):
-            copy(noisy.at[first + n], planes.at[d, pl.ds(n * size, size)], 8 + own * d + n)
+            copy(noisy.at[first + n], to.at[pl.ds(n * size, size)], 8 + own * d + n)
     for c in copies[:6]:
         c.wait()
     for d in range(2):
@@ -408,13 +410,9 @@
             mid = left.astype(BF16)
             low = (left - mid.astype(F32)).astype(BF16)
             for plane in (seen, which, high, mid, low):
-                planes[d, at : at + rows, :] = plane
+                ends[d][0][at : at + rows, :] = plane
                 at += rows
-    for d in range(2):
-        for c in copies[6 + own * d : 6 + own * (d + 1)]:
-            c.wait()
-        copy(planes.at[d], ends[d][0], 4 * d + 3)
-    for c in copies[-2:]:
+    for c in copies[6:]:
         c.wait()
 
 
@@ -467,10 +465,13 @@
         def keep(at, x):
             nperm[f, at : at + x.shape[0], :] = x.astype(BF16)
 
-        return (lambda: noisy_s[f]), f, keep
-
-    for c in arriving[: frames // 2]:
-        c.wait()
+        def source():
+            if m == 0:
+                arriving[j].wait()
+            return noisy_s[f]
+
+        return source, f, keep
+
     reorder_frames(dims, units, c_in, perm, wide, jobs, frames // 2)
     leave(wide, wide_out)
     leave(nperm, nperm_out)
@@ -490,10 +491,10 @@
 
 
 def outer_kernel(
-    dims, step, b2s, obs, mask, chan, before, after,
+    dims, step, b2s, obs, mask, chan, before_s, after_s,
     wide_in, nperm_in, grads_in, rest_in, w1_in, w2_in, w2t_in, wt1_in,
     out,
-    w1, w2, w2t, wt1, perm, wide, nperm, before_s, after_s, seen, which, value, deriv0, deriv1, part0, part1, acts, mis,
+    w1, w2, w2t, wt1, perm, wide, nperm, seen, which, value, deriv0, deriv1, part0, part1, acts, mis,
     grads, rest, qs, stage, result, sems,
 ):
     frames, chans, rows, cols, hid, span = dims
@@ -516,8 +517,6 @@
         copies.append(Copy(make))
         copies[-1].start()
 
-    arrive(before, before_s)
-    arrive(after, after_s)
     for a, b in ((mask, seen), (chan, which), (obs, value)):
         arrive(a, b, 0, half, half)
         arrive(a, b, frames - half, 2 * half, half)
@@ -540,14 +539,11 @@
         place = 3 * half + j if m else j - half
 
         def keep(at, x):
-            @pl.when(keeps)
-            def _():
+            if keeps:
                 nperm[place, at : at + x.shape[0], :] = x.astype(BF16)
 
-        return (lambda: src[pl.ds(pl.multiple_of(j * size, size), size), :]), slot, keep
-
-    copies[0].wait()
-    copies[1].wait()
+        return (lambda: src[j * size : (j + 1) * size, :]), slot, keep
+
     for n in range(half):
         for src, base in ((before_s, 0), (after_s, 3 * half)):
             at = own * size + 5 * rows * n
@@ -556,7 +552,7 @@
             which[base + n] = planes[1].astype(jnp.int32)
             value[base + n] = planes[2] + (planes[3] + planes[4])
     reorder_frames(dims, units, c_in, perm, wide, jobs, own)
-    for copy in copies[2:early]:
+    for copy in copies[:early]:
         copy.wait()
 
     def where(i):
@@ -617,20 +613,18 @@
     planes = 2 * half * size + 5 * half * rows
     to_up, to_down = pl.pallas_call(
         functools.partial(pack_kernel, dims),
-        out_shape=(shape((planes, cols), BF16), shape((planes, cols), BF16)),
+        out_shape=(pltpu.VMEM((planes, cols), BF16), pltpu.VMEM((planes, cols), BF16)),
         in_specs=[hbm] * 4,
-        out_specs=(hbm, hbm),
+        out_specs=(vmem, vmem),
         scratch_shapes=[
-            pltpu.VMEM((2, planes, cols), BF16),
             pltpu.VMEM((2, half, rows, cols), F32),
             pltpu.VMEM((2, half, rows, cols), jnp.int32),
             pltpu.VMEM((2, half, rows, cols), jnp.int32),
             pltpu.SemaphoreType.DMA((8 + 4 * half,)),
         ],
-        compiler_params=pltpu.CompilerParams(vmem_limit_bytes=62 << 20),
     )(flat, observed, obs_mask, obs_channel)
-    before = pltpu.with_memory_space_constraint(lax.ppermute(to_up, "tm", up), pltpu.HBM)
-    after = pltpu.with_memory_space_constraint(lax.ppermute(to_down, "tm", down), pltpu.HBM)
+    before = pltpu.with_memory_space_constraint(lax.ppermute(to_up, "tm", up), pltpu.VMEM)
+    after = pltpu.with_memory_space_constraint(lax.ppermute(to_down, "tm", down), pltpu.VMEM)
 
     wf = jnp.transpose(w_first, (2, 3, 1, 0)).reshape(9 * span * chans, hid)
     ws = jnp.transpose(w_second, (2, 3, 0, 1)).reshape(9 * chans, hid)
@@ -674,15 +668,13 @@
     out = pl.pallas_call(
         functools.partial(outer_kernel, dims),
         out_shape=shape((frames, size, cols), F32),
-        in_specs=[smem, smem] + [hbm] * 13,
+        in_specs=[smem, smem] + [hbm] * 3 + [vmem] * 2 + [hbm] * 8,
         out_specs=hbm,
         scratch_shapes=[pltpu.VMEM(*w) for w in weights]
         + [
             pltpu.VMEM((size, size), BF16),
             pltpu.VMEM((frames + 4 * half, wide_rows, cols), BF16),
             pltpu.VMEM((4 * half, size, cols), BF16),
-            pltpu.VMEM((planes, cols), BF16),
-            pltpu.VMEM((planes, cols), BF16),
             pltpu.VMEM((4 * half, rows, cols), jnp.int32),
             pltpu.VMEM((4 * half, rows, cols), jnp.int32),
             pltpu.VMEM((4 * half, rows, cols), F32),
@@ -696,7 +688,7 @@
             pltpu.VMEM((frames, size, cols), F32),
             pltpu.SemaphoreType.DMA((16 + frames + frames // 2,)),
         ],
-        compiler_params=pltpu.CompilerParams(vmem_limit_bytes=62 << 20),
+        compiler_params=pltpu.CompilerParams(vmem_limit_bytes=56 << 20),
     )(step_index, b_second, observed, obs_mask, obs_channel, before, after, *results)
     return out.reshape(frames, chans, rows, cols)
 

time: 52.6 us -> 46.9 us (0.89)
  Pallas kernels: 44 us -> 38.9 us
  local copies, waits for them, and re-layouts: 1.02 us -> 0 us
    pallas_call x1, Pallas kernels: 29 us -> 25.2 us  [per_device(): pl.pallas_call(functools.partial(outer_kernel, dims), out_shape=shape((fr...]
    pallas_call x1, Pallas kernels: 12.6 us -> 11.4 us  [per_device(): pl.pallas_call(functools.partial(inner_kernel, dims), out_shape=tuple((sh...]
    unnamed x4 -> x0, local copies, waits for them, and re-layouts: 1.02 us -> none
  transfers between devices with their start and end apart: 2 -> 2, of which waited for: 0 -> 0; matrix products, arithmetic and copies ran while one was open for 0% -> 0% of each run, Pallas kernels for 24% -> 25%
where the time goes in v4:
time: 46.9 us; the launch traced here: 46.2 us
  Pallas kernels  38.9 us (83%)
  starting transfers between devices  6.43 us (14%)
  between operations  0.88 us (2%)
    pallas_call x1, Pallas kernels, per_device(): pl.pallas_call(functools.partial(outer_kernel, dims), out_shape=shape((fr...  25.2 us
    pallas_call x1, Pallas kernels, per_device(): pl.pallas_call(functools.partial(inner_kernel, dims), out_shape=tuple((sh...  11.4 us
    ppermute x1, starting transfers between devices, per_device(): lax.ppermute(to_up, 'tm', up)  4.51 us
    pallas_call x1, Pallas kernels, per_device(): pl.pallas_call(functools.partial(pack_kernel, dims), out_shape=(pltpu.VME...  2.33 us
    ppermute x1, starting transfers between devices, per_device(): lax.ppermute(to_down, 'tm', down)  1.92 us
  transfers between devices with their start and end apart: 2, of which 0 were waited for; matrix products, arithmetic and copies ran while one was open for 0% of the time, Pallas kernels for 25%

profile of v4, /device:TPU:1, one launch (start us, length us, event | category | flops | bytes accessed | tf_op | source)
XLA Modules:
  0.0 46.2 jit_solution(5935005270053959762)
XLA Ops:
  0.0 2.3 %shard_map.91 = (bf16[1184,256]{1,0:T(8,128)(2,1)}, bf16[1184,256]{1,0:T(8,128)(2,1)S(1)}) custom-call(bf16[8,256,256]{2,1,0:T(8,128)(2,1)} %bitcast.9, f32[8,16,256]{2,1,0:T(8,128)} %obs.5, s32[8,16,256]{2,1,0:T(8,128)} %mask.5, s32[8,16,256]{2,1,0:T(8,128)} %chan.5), custom_call_target="tpu_custom_call" | custom-call | tf_op jit(solution)/shard_map/pallas_call | solution.py:614
  2.3 4.5 %collective-permute-start = (bf16[1184,256]{1,0:T(8,128)(2,1)}, bf16[1184,256]{1,0:T(8,128)(2,1)S(1)}, u32[]{:S(2)}, u32[]{:S(2)}) collective-permute-start(bf16[1184,256]{1,0:T(8,128)(2,1)} %get-tuple-element.15), channel_id=1, source_target_pairs={{0,1},{1,2},{2,3},{3,4},{4,5},{5,6},{6,7},{7,8},{8,9},{9,10},{10,1... | collective-permute-start | bytes 1818632 | tf_op jit(solution)/shard_map/ppermute | solution.py:626
  6.9 1.9 %collective-permute-start.1 = (bf16[1184,256]{1,0:T(8,128)(2,1)S(1)}, bf16[1184,256]{1,0:T(8,128)(2,1)S(1)}, u32[]{:S(2)}, u32[]{:S(2)}) collective-permute-start(bf16[1184,256]{1,0:T(8,128)(2,1)S(1)} %get-tuple-element.16), channel_id=1, source_target_pairs={{1,0},{2,1},{3,2},{4,3},{5,4},{6,5},{7,6},{8,7},{9,8},{10,9},{11,1... | collective-permute-start | bytes 1818632 | tf_op jit(solution)/shard_map/ppermute | solution.py:627
  9.4 11.4 %shard_map.92 = (bf16[8,864,256]{2,1,0:T(8,128)(2,1)}, bf16[8,256,256]{2,1,0:T(8,128)(2,1)}, bf16[4,16,128,256]{3,2,1,0:T(8,128)(2,1)}, f32[4,256,256]{2,1,0:T(8...) custom-call(s32[1]{0:T(128)S(6)} %copy.10.step, ...), custom_call_target="tpu_custom_call" | custom-call | flops 16911433728 | bytes 12582912 | tf_op jit(solution)/shard_map/pallas_call | solution.py:653
  20.8 0.0 collective-permute-done.before_s
  20.8 0.0 collective-permute-done.1.after_s
  20.8 25.2 %shard_map.93 = f32[8,256,256]{2,1,0:T(8,128)} custom-call(s32[1]{0:T(128)S(6)} %copy.10.step, f32[16]{0:T(128)} %b2s.3, f32[8,16,256]{2,1,0:T(8,128)} %obs.5, s32[8,16,256]{2,1,0:T(8,128)} %mask.5, s32[8,16,256]{2,1,0:T(8,128)} %chan.5, bf16[1184,256]{1,0:T(8,128)(2,1)S(1)} %collective-permute-done.before_s, ...), custom_call_target="tpu_custom_call" | custom-call | tf_op jit(solution)/shard_map/pallas_call | solution.py:668
Async XLA Ops:
  2.3 18.5 %collective-permute-start = (bf16[1184,256]{1,0:T(8,128)(2,1)}, bf16[1184,256]{1,0:T(8,128)(2,1)S(1)}, u32[]{:S(2)}, u32[]{:S(2)}) collective-permute-start(bf16[1184,256]{1,0:T(8,128)(2,1)} %get-tuple-element.15), channel_id=1, source_target_pairs={{0,1},{1,2},{2,3},{3,4},{4,5},{5,6},{6,7},{7,8},{8,9},{9,10},{10,1... | collective-permute-start | bytes 1818632 | tf_op jit(solution)/shard_map/ppermute | solution.py:626
  6.9 14.0 %collective-permute-start.1 = (bf16[1184,256]{1,0:T(8,128)(2,1)S(1)}, bf16[1184,256]{1,0:T(8,128)(2,1)S(1)}, u32[]{:S(2)}, u32[]{:S(2)}) collective-permute-start(bf16[1184,256]{1,0:T(8,128)(2,1)S(1)} %get-tuple-element.16), channel_id=1, source_target_pairs={{1,0},{2,1},{3,2},{4,3},{5,4},{6,5},{7,6},{8,7},{9,8},{10,9},{11,1... | collective-permute-start | bytes 1818632 | tf_op jit(solution)/shard_map/ppermute | solution.py:627

commit v5 on v4

--- a/solution.py
+++ b/solution.py
@@ -13,7 +13,7 @@
 sigma_ratio = 20.0
 F32 = jnp.float32
 BF16 = jnp.bfloat16
-CHUNK = 32
+CHUNK = 64
 
 
 def shifted(x, by):

time: 46.9 us -> 46.9 us (level)
  no operation moved by 1% of the time
where the time goes in v5:
time: 46.9 us; the launch traced here: 46.3 us
  Pallas kernels  38.9 us (83%)
  starting transfers between devices  6.43 us (14%)
  between operations  0.88 us (2%)
    pallas_call x1, Pallas kernels, per_device(): pl.pallas_call(functools.partial(outer_kernel, dims), out_shape=shape((fr...  25.2 us
    pallas_call x1, Pallas kernels, per_device(): pl.pallas_call(functools.partial(inner_kernel, dims), out_shape=tuple((sh...  11.4 us
    ppermute x1, starting transfers between devices, per_device(): lax.ppermute(to_up, 'tm', up)  4.51 us
    pallas_call x1, Pallas kernels, per_device(): pl.pallas_call(functools.partial(pack_kernel, dims), out_shape=(pltpu.VME...  2.33 us
    ppermute x1, starting transfers between devices, per_device(): lax.ppermute(to_down, 'tm', down)  1.92 us
  transfers between devices with their start and end apart: 2, of which 0 were waited for; matrix products, arithmetic and copies ran while one was open for 0% of the time, Pallas kernels for 25%

profile of v5, /device:TPU:1, one launch (start us, length us, event | category | flops | bytes accessed | tf_op | source)
XLA Modules:
  0.0 46.3 jit_solution(10360408940542930468)
XLA Ops:
  0.0 2.3 %shard_map.91 = (bf16[1184,256]{1,0:T(8,128)(2,1)}, bf16[1184,256]{1,0:T(8,128)(2,1)S(1)}) custom-call(bf16[8,256,256]{2,1,0:T(8,128)(2,1)} %bitcast.9, f32[8,16,256]{2,1,0:T(8,128)} %obs.5, s32[8,16,256]{2,1,0:T(8,128)} %mask.5, s32[8,16,256]{2,1,0:T(8,128)} %chan.5), custom_call_target="tpu_custom_call" | custom-call | tf_op jit(solution)/shard_map/pallas_call | solution.py:614
  2.3 4.5 %collective-permute-start = (bf16[1184,256]{1,0:T(8,128)(2,1)}, bf16[1184,256]{1,0:T(8,128)(2,1)S(1)}, u32[]{:S(2)}, u32[]{:S(2)}) collective-permute-start(bf16[1184,256]{1,0:T(8,128)(2,1)} %get-tuple-element.15), channel_id=1, source_target_pairs={{0,1},{1,2},{2,3},{3,4},{4,5},{5,6},{6,7},{7,8},{8,9},{9,10},{10,1... | collective-permute-start | bytes 1818632 | tf_op jit(solution)/shard_map/ppermute | solution.py:626
  6.9 1.9 %collective-permute-start.1 = (bf16[1184,256]{1,0:T(8,128)(2,1)S(1)}, bf16[1184,256]{1,0:T(8,128)(2,1)S(1)}, u32[]{:S(2)}, u32[]{:S(2)}) collective-permute-start(bf16[1184,256]{1,0:T(8,128)(2,1)S(1)} %get-tuple-element.16), channel_id=1, source_target_pairs={{1,0},{2,1},{3,2},{4,3},{5,4},{6,5},{7,6},{8,7},{9,8},{10,9},{11,1... | collective-permute-start | bytes 1818632 | tf_op jit(solution)/shard_map/ppermute | solution.py:627
  9.4 11.4 %shard_map.92 = (bf16[8,864,256]{2,1,0:T(8,128)(2,1)}, bf16[8,256,256]{2,1,0:T(8,128)(2,1)}, bf16[4,16,128,256]{3,2,1,0:T(8,128)(2,1)}, f32[4,256,256]{2,1,0:T(8...) custom-call(s32[1]{0:T(128)S(6)} %copy.10.step, ...), custom_call_target="tpu_custom_call" | custom-call | flops 16911433728 | bytes 12582912 | tf_op jit(solution)/shard_map/pallas_call | solution.py:653
  20.8 0.0 collective-permute-done.before_s
  20.8 0.0 collective-permute-done.1.after_s
  20.9 25.2 %shard_map.93 = f32[8,256,256]{2,1,0:T(8,128)} custom-call(s32[1]{0:T(128)S(6)} %copy.10.step, f32[16]{0:T(128)} %b2s.3, f32[8,16,256]{2,1,0:T(8,128)} %obs.5, s32[8,16,256]{2,1,0:T(8,128)} %mask.5, s32[8,16,256]{2,1,0:T(8,128)} %chan.5, bf16[1184,256]{1,0:T(8,128)(2,1)S(1)} %collective-permute-done.before_s, ...), custom_call_target="tpu_custom_call" | custom-call | tf_op jit(solution)/shard_map/pallas_call | solution.py:668
Async XLA Ops:
  2.3 18.5 %collective-permute-start = (bf16[1184,256]{1,0:T(8,128)(2,1)}, bf16[1184,256]{1,0:T(8,128)(2,1)S(1)}, u32[]{:S(2)}, u32[]{:S(2)}) collective-permute-start(bf16[1184,256]{1,0:T(8,128)(2,1)} %get-tuple-element.15), channel_id=1, source_target_pairs={{0,1},{1,2},{2,3},{3,4},{4,5},{5,6},{6,7},{7,8},{8,9},{9,10},{10,1... | collective-permute-start | bytes 1818632 | tf_op jit(solution)/shard_map/ppermute | solution.py:626
  6.9 14.0 %collective-permute-start.1 = (bf16[1184,256]{1,0:T(8,128)(2,1)S(1)}, bf16[1184,256]{1,0:T(8,128)(2,1)S(1)}, u32[]{:S(2)}, u32[]{:S(2)}) collective-permute-start(bf16[1184,256]{1,0:T(8,128)(2,1)S(1)} %get-tuple-element.16), channel_id=1, source_target_pairs={{1,0},{2,1},{3,2},{4,3},{5,4},{6,5},{7,6},{8,7},{9,8},{10,9},{11,1... | collective-permute-start | bytes 1818632 | tf_op jit(solution)/shard_map/ppermute | solution.py:627
